TPU v7x, 768 devices: a whole 4x8x12 slice. The times are simulated.
768 devices in a mesh: len: 96 (over x, z, y_hi), xs: 8 (over y_lo, core).
Axes of the slice: x: 4, y: 8 (y_hi: 2, y_lo: 4; y = y_hi * 4 + y_lo), z: 12, core: 2. Of those that a mesh axis runs over, the one named last changes fastest.
Arguments:
- alpha: float32 [768, 256, 256], P('len', 'xs'), may hold values from 0 to 1
- velocity: float32 [3, 768, 256, 256], P(None, 'len', 'xs'), may hold values from -4 to 4
- upwind: int32 [3, 768, 256, 256], P(None, 'len', 'xs'), may hold values 0 or 1
- celltype: int32 [768, 256, 256], P('len', 'xs'), may hold values from 0 to 3
- owner: int32 [256, 256], P('xs'), may hold values from 0 to 15
- lam_alpha: float32 [768, 256, 256], P('len', 'xs'), may hold values from -6 to 6
- lam_press: float32 [768, 256, 256], P('len', 'xs'), may hold values from -6 to 6
Outputs:
- grad_alpha: float32 [768, 256, 256], P('len', 'xs')
- grad_velocity: float32 [3, 768, 256, 256], P(None, 'len', 'xs')
- adjoint_pressure: float32 [768, 256, 256], P('len', 'xs')
- inlet_sens: float32 [16], replicated
Inputs may be any that keep to these rules, and one draw needn't show every extreme that they name: `celltype`: cell type codes. `owner`: port indices.
All inputs are finite; a program needn't handle non-finite values. No bound on the sum of `upwind` on one device may be relied on, other than what follows from the above.
Results may differ from a plain program's by a relative error of at most 0.00024.
Values sent between devices are 32-bit elements; how exact they have to be, the bound alone decides.
No kernel may reach another device: no remote copies, remote signals or barrier semaphores. Data moves between devices by JAX's collectives and lax.ppermute only.
A program may use at most 32 MiB of HBM per device.

v0:
```python
import math

import jax
import jax.numpy as jnp
from jax import lax
from jax.sharding import PartitionSpec as P

SWEEPS = 2
PORTS = 16


def with_halo(x, sides, width):
    for axis, dim in sides:
        count, length = (lax.axis_size(axis), x.shape[dim])
        up = [(i, (i + 1) % count) for i in range(count - 1)]
        down = [(j, i) for i, j in up]
        last = lax.slice_in_dim(x, length - width, length, axis=dim)
        leading = lax.slice_in_dim(x, 0, width, axis=dim)
        before = lax.ppermute(last, axis, up)
        after = lax.ppermute(leading, axis, down)
        x = jnp.concatenate([before, x, after], axis=dim)
    return x


def from_behind(x, axis, by):
    count = lax.axis_size(axis)
    pairs = [(i, i + by) for i in range(count) if 0 <= i + by < count]
    return lax.ppermute(x, axis, pairs)


def widen(padded):
    pads = [(0, 0)] * (padded.ndim - 1) + [(1, 1)]
    return jnp.pad(padded, pads)


def pick(wide, axis, offset, shape):
    starts = [1, 1, 1]
    starts[axis] = starts[axis] + offset
    return wide[
        ...,
        starts[0] : starts[0] + shape[0],
        starts[1] : starts[1] + shape[1],
        starts[2] : starts[2] + shape[2],
    ]


def relax(press, rhs, diag, active, k_high, k_low):
    padded = with_halo(press, (("len", 0), ("xs", 1)), 1)
    wide = widen(padded)
    shape = press.shape
    beside = k_high[0] * pick(wide, 0, 1, shape) + k_low[0] * pick(wide, 0, -1, shape)
    beside = beside + k_high[1] * pick(wide, 1, 1, shape) + k_low[1] * pick(wide, 1, -1, shape)
    beside = beside + k_high[2] * pick(wide, 2, 1, shape) + k_low[2] * pick(wide, 2, -1, shape)
    return active * (rhs + beside) / diag


def body(alpha, velocity, upwind, celltype, owner, lam_alpha, lam_press):
    shape = alpha.shape
    opened = (celltype != 1).astype(jnp.float32)
    active = ((celltype == 0) | (celltype == 2)).astype(jnp.float32)
    inlet = (celltype == 2).astype(jnp.float32)
    flows = upwind.astype(jnp.float32)
    rho = 1.0 + 9.0 * alpha
    stacked = jnp.stack([alpha, lam_alpha, opened])
    padded = with_halo(stacked, (("len", 1), ("xs", 2)), 1)
    wide = widen(padded)
    total = lam_alpha
    grads = []
    k_high = []
    k_low = []
    for axis in range(3):
        flow = flows[axis]
        after = pick(wide, axis, 1, shape)
        before = pick(wide, axis, -1, shape)
        alpha_next, lam_next, open_next = (after[0], after[1], after[2])
        alpha_prev, lam_prev, open_prev = (before[0], before[1], before[2])
        face = 0.4 * velocity[axis] * (lam_next - lam_alpha) * (opened * open_next)
        grads.append(face * (flow * alpha + (1.0 - flow) * alpha_next))
        passed = face * (1.0 - flow)
        if axis == 2:
            incoming = jnp.pad(passed, ((0, 0), (0, 0), (1, 0)))[:, :, :-1]
        elif axis == 0:
            edge = from_behind(passed[-1:], "len", 1)
            incoming = jnp.concatenate([edge, passed[:-1]], axis=0)
        else:
            edge = from_behind(passed[:, -1:], "xs", 1)
            incoming = jnp.concatenate([edge, passed[:, :-1]], axis=1)
        total = total + face * flow + incoming
        k_high.append(2.0 * (opened * open_next) / (rho + (1.0 + 9.0 * alpha_next)))
        k_low.append(2.0 * (open_prev * opened) / (1.0 + 9.0 * alpha_prev + rho))
    grad_alpha = opened * total
    grad_velocity = jnp.stack(grads)
    diag = 0.5 + (k_high[0] + k_high[1] + k_high[2]) + (k_low[0] + k_low[1] + k_low[2])
    rhs = lam_press + grad_alpha
    press = active * rhs / diag
    for sweep in range(SWEEPS):
        press = relax(press, rhs, diag, active, k_high, k_low)
    column = jnp.sum((lam_alpha + press) * inlet, axis=0)
    ports = jnp.arange(PORTS, dtype=jnp.int32)
    partial_sens = jnp.sum(
        jnp.where(owner[None] == ports[:, None, None], column[None], 0.0), axis=(1, 2)
    )
    summed = lax.psum(partial_sens, ("len", "xs"))
    cells = shape[0] * shape[1] * shape[2] * lax.axis_size("len") * lax.axis_size("xs")
    sens = summed / math.sqrt(cells)
    return (grad_alpha, grad_velocity, press, sens)


def solution(mesh):
    in_specs = (
        P("len", "xs", None),
        P(None, "len", "xs", None),
        P(None, "len", "xs", None),
        P("len", "xs", None),
        P("xs", None),
        P("len", "xs", None),
        P("len", "xs", None),
    )
    out_specs = (P("len", "xs", None), P(None, "len", "xs", None), P("len", "xs", None), P())
    return jax.shard_map(body, mesh=mesh, in_specs=in_specs, out_specs=out_specs, check_vma=False)
```

profile of v0, /device:TPU:1, one launch (start us, length us, event | category | flops | bytes accessed | tf_op | source)
XLA Modules:
  0.0 212.0 jit_solution(15585608258122729949)
XLA Ops:
  0.6 1.1 convert_bitcast_fusion
  1.7 0.0 copy-start
  1.7 0.0 copy-start.1
  1.7 0.0 copy-start.3
  1.8 0.9 pad_maximum_fusion.33
  2.7 8.3 %collective-permute-start.2 = (f32[3,1,32,256]{3,2,1,0:T(8,128)S(1)}, f32[3,1,32,256]{3,2,1,0:T(8,128)S(1)}, u32[]{:S(2)}, u32[]{:S(2)}) collective-permute-start(f32[3,1,32,256]{3,2,1,0:T(8,128)S(1)} %get-tuple-element.28), channel_id=1, source_target_pairs={{0,8},{8,16},{16,24},{24,32},{32,40},{40,48},{48,56},{56,64},{64,7... | collective-permute-start | bytes 294920 | tf_op jit(solution)/shard_map/ppermute | solution.py:19
  11.0 1.3 collective-permute-start
  12.3 0.3 collective-permute-done.2
  12.6 7.8 %collective-permute-done = f32[3,1,32,256]{3,2,1,0:T(8,128)S(1)} collective-permute-done((f32[3,1,32,256]{3,2,1,0:T(8,128)S(1)}, f32[3,1,32,256]{3,2,1,0:T(8,128)S(1)}, u32[]{:S(2)}, u32[]{:S(2)}) %collective-permute-start) | collective-permute-done | bytes 98336 | tf_op jit(solution)/shard_map/ppermute | solution.py:20
  20.3 1.0 pad_maximum_fusion.36
  21.3 10.0 %collective-permute-start.3 = (f32[3,10,1,256]{3,2,1,0:T(1,128)S(1)}, f32[3,10,1,256]{3,2,1,0:T(1,128)S(1)}, u32[]{:S(2)}, u32[]{:S(2)}) collective-permute-start(f32[3,10,1,256]{3,2,1,0:T(1,128)S(1)} %get-tuple-element.25), channel_id=1, source_target_pairs={{1,0},{2,1},{3,2},{4,3},{5,4},{6,5},{7,6},{9,8},{10,9},{11,10},{12... | collective-permute-start | bytes 92168 | tf_op jit(solution)/shard_map/ppermute | solution.py:20
  31.3 0.1 convert_element_type.8
  31.4 1.9 collective-permute-start.5
  33.3 0.0 collective-permute-done.3
  33.4 0.2 multiply_bitcast_fusion.1
  33.6 0.3 multiply_bitcast_fusion.2
  33.9 1.9 collective-permute-start.4
  35.8 0.0 collective-permute-done.5
  35.8 0.8 select_maximum_fusion
  36.6 0.0 copy-start.2
  36.6 0.0 copy-start.5
  36.6 0.3 multiply_bitcast_fusion
  37.0 1.3 collective-permute-start.1
  38.4 0.0 collective-permute-done.4
  38.4 0.9 collective-permute-done.1
  39.3 1.7 fusion.65
  41.0 7.5 %collective-permute-start.7 = (f32[1,32,256]{2,1,0:T(8,128)S(1)}, f32[1,32,256]{2,1,0:T(8,128)S(1)}, u32[]{:S(2)}, u32[]{:S(2)}) collective-permute-start(f32[1,32,256]{2,1,0:T(8,128)S(1)} %get-tuple-element.36), channel_id=1, source_target_pairs={{0,8},{8,16},{16,24},{24,32},{32,40},{40,48},{48,56},{56,64},{64,7... | collective-permute-start | bytes 98312 | tf_op jit(solution)/shard_map/ppermute | solution.py:19
  48.5 1.3 collective-permute-start.6
  49.8 7.7 %collective-permute-done.6 = f32[1,32,256]{2,1,0:T(8,128)S(1)} collective-permute-done((f32[1,32,256]{2,1,0:T(8,128)S(1)}, f32[1,32,256]{2,1,0:T(8,128)S(1)}, u32[]{:S(2)}, u32[]{:S(2)}) %collective-permute-start.6) | collective-permute-done | bytes 32800 | tf_op jit(solution)/shard_map/ppermute | solution.py:20
  57.6 6.3 %collective-permute-start.9 = (f32[10,1,256]{2,1,0:T(1,128)S(1)}, f32[10,1,256]{2,1,0:T(1,128)S(1)}, u32[]{:S(2)}, u32[]{:S(2)}) collective-permute-start(f32[10,1,256]{2,1,0:T(1,128)S(1)} %get-tuple-element.32), channel_id=1, source_target_pairs={{0,1},{1,2},{2,3},{3,4},{4,5},{5,6},{6,7},{8,9},{9,10},{10,11},{11... | collective-permute-start | bytes 30728 | tf_op jit(solution)/shard_map/ppermute | solution.py:19
  63.9 1.9 collective-permute-start.8
  65.8 0.0 collective-permute-done.9
  65.8 3.1 %collective-permute-done.8 = f32[10,1,256]{2,1,0:T(1,128)S(1)} collective-permute-done((f32[10,1,256]{2,1,0:T(1,128)S(1)}, f32[10,1,256]{2,1,0:T(1,128)S(1)}, u32[]{:S(2)}, u32[]{:S(2)}) %collective-permute-start.8) | collective-permute-done | bytes 10272 | tf_op jit(solution)/shard_map/ppermute | solution.py:20
  68.9 0.3 select_maximum_fusion.10
  69.2 0.3 fusion.19
  69.5 6.9 %collective-permute-start.11 = (f32[1,32,256]{2,1,0:T(8,128)S(1)}, f32[1,32,256]{2,1,0:T(8,128)S(1)}, u32[]{:S(2)}, u32[]{:S(2)}) collective-permute-start(f32[1,32,256]{2,1,0:T(8,128)S(1)} %get-tuple-element.34), channel_id=1, source_target_pairs={{0,8},{8,16},{16,24},{24,32},{32,40},{40,48},{48,56},{56,64},{64,7... | collective-permute-start | bytes 98312 | tf_op jit(solution)/shard_map/ppermute | solution.py:19
  76.4 1.3 collective-permute-start.10
  77.8 7.3 %collective-permute-done.10 = f32[1,32,256]{2,1,0:T(8,128)S(1)} collective-permute-done((f32[1,32,256]{2,1,0:T(8,128)S(1)}, f32[1,32,256]{2,1,0:T(8,128)S(1)}, u32[]{:S(2)}, u32[]{:S(2)}) %collective-permute-start.10) | collective-permute-done | bytes 32800 | tf_op jit(solution)/shard_map/ppermute | solution.py:20
  85.0 3.7 %collective-permute-start.13 = (f32[10,1,256]{2,1,0:T(1,128)S(1)}, f32[10,1,256]{2,1,0:T(1,128)S(1)}, u32[]{:S(2)}, u32[]{:S(2)}) collective-permute-start(f32[10,1,256]{2,1,0:T(1,128)S(1)} %get-tuple-element.30), channel_id=1, source_target_pairs={{0,1},{1,2},{2,3},{3,4},{4,5},{5,6},{6,7},{8,9},{9,10},{10,11},{11... | collective-permute-start | bytes 30728 | tf_op jit(solution)/shard_map/ppermute | solution.py:19
  88.8 1.9 collective-permute-start.12
  90.7 3.1 %collective-permute-done.12 = f32[10,1,256]{2,1,0:T(1,128)S(1)} collective-permute-done((f32[10,1,256]{2,1,0:T(1,128)S(1)}, f32[10,1,256]{2,1,0:T(1,128)S(1)}, u32[]{:S(2)}, u32[]{:S(2)}) %collective-permute-start.12) | collective-permute-done | bytes 10272 | tf_op jit(solution)/shard_map/ppermute | solution.py:20
  93.8 0.3 select_maximum_fusion.6
  94.1 0.0 copy-start.6
  94.1 1.1 select_reduce_fusion.1
  95.2 0.2 select_reduce_fusion
  95.4 1.0 pad_maximum_fusion
  96.4 115.1 %psum.7 = f32[16]{0:T(128)S(1)} all-reduce(f32[16]{0:T(128)S(1)} %select_reduce_fusion), channel_id=1, replica_groups=mesh['len'=96,'xs'=8] {'len','xs'}, use_global_device_ids=true, to_apply=%region_2.3 | all-reduce | flops 16 | bytes 128 | tf_op jit(solution)/shard_map/psum | solution.py:103
  211.4 0.5 broadcast_multiply_fusion
  (19 shorter events, 0.1 us)
Async XLA Ops:
  0.6 30.7 %copy-start.4 = (s32[3,8,32,256]{3,2,1,0:T(8,128)S(1)}, s32[3,8,32,256]{3,2,1,0:T(8,128)}, u32[]{:S(2)}) copy-start(s32[3,8,32,256]{3,2,1,0:T(8,128)} %param.9) | copy-start | bytes 2359300
  1.7 31.6 %copy-start = (f32[8,32,256]{2,1,0:T(8,128)S(1)}, f32[8,32,256]{2,1,0:T(8,128)}, u32[]{:S(2)}) copy-start(f32[8,32,256]{2,1,0:T(8,128)} %param.12) | copy-start | bytes 786436
  1.7 31.6 %copy-start.1 = (f32[8,32,256]{2,1,0:T(8,128)S(1)}, f32[8,32,256]{2,1,0:T(8,128)}, u32[]{:S(2)}) copy-start(f32[8,32,256]{2,1,0:T(8,128)} %param.7) | copy-start | bytes 786436
  1.7 31.6 %copy-start.3 = (f32[3,8,32,256]{3,2,1,0:T(8,128)S(1)}, f32[3,8,32,256]{3,2,1,0:T(8,128)}, u32[]{:S(2)}) copy-start(f32[3,8,32,256]{3,2,1,0:T(8,128)} %param.8) | copy-start | bytes 2359300
  2.7 9.9 %collective-permute-start.2 = (f32[3,1,32,256]{3,2,1,0:T(8,128)S(1)}, f32[3,1,32,256]{3,2,1,0:T(8,128)S(1)}, u32[]{:S(2)}, u32[]{:S(2)}) collective-permute-start(f32[3,1,32,256]{3,2,1,0:T(8,128)S(1)} %get-tuple-element.28), channel_id=1, source_target_pairs={{0,8},{8,16},{16,24},{24,32},{32,40},{40,48},{48,56},{56,64},{64,7... | collective-permute-start | bytes 294920 | tf_op jit(solution)/shard_map/ppermute | solution.py:19
  11.0 9.4 %collective-permute-start = (f32[3,1,32,256]{3,2,1,0:T(8,128)S(1)}, f32[3,1,32,256]{3,2,1,0:T(8,128)S(1)}, u32[]{:S(2)}, u32[]{:S(2)}) collective-permute-start(f32[3,1,32,256]{3,2,1,0:T(8,128)S(1)} %get-tuple-element.29), channel_id=1, source_target_pairs={{8,0},{16,8},{24,16},{32,24},{40,32},{48,40},{56,48},{64,56},{72,6... | collective-permute-start | bytes 294920 | tf_op jit(solution)/shard_map/ppermute | solution.py:20
  21.3 12.0 %collective-permute-start.3 = (f32[3,10,1,256]{3,2,1,0:T(1,128)S(1)}, f32[3,10,1,256]{3,2,1,0:T(1,128)S(1)}, u32[]{:S(2)}, u32[]{:S(2)}) collective-permute-start(f32[3,10,1,256]{3,2,1,0:T(1,128)S(1)} %get-tuple-element.25), channel_id=1, source_target_pairs={{1,0},{2,1},{3,2},{4,3},{5,4},{6,5},{7,6},{9,8},{10,9},{11,10},{12... | collective-permute-start | bytes 92168 | tf_op jit(solution)/shard_map/ppermute | solution.py:20
  31.4 4.4 %collective-permute-start.5 = (f32[3,10,1,256]{3,2,1,0:T(1,128)S(1)}, f32[3,10,1,256]{3,2,1,0:T(1,128)S(1)}, u32[]{:S(2)}, u32[]{:S(2)}) collective-permute-start(f32[3,10,1,256]{3,2,1,0:T(1,128)S(1)} %get-tuple-element.24), channel_id=1, source_target_pairs={{0,1},{1,2},{2,3},{3,4},{4,5},{5,6},{6,7},{8,9},{9,10},{10,11},{11... | collective-permute-start | bytes 92168 | tf_op jit(solution)/shard_map/ppermute | solution.py:19
  33.9 4.5 %collective-permute-start.4 = (f32[8,1,256]{2,1,0:T(1,128)S(1)}, f32[8,1,256]{2,1,0:T(1,128)S(1)}, u32[]{:S(2)}, u32[]{:S(2)}) collective-permute-start(f32[8,1,256]{2,1,0:T(1,128)S(1)} %slice.262), channel_id=1, source_target_pairs={{0,1},{1,2},{2,3},{3,4},{4,5},{5,6},{6,7},{8,9},{9,10},{10,11},{11... | collective-permute-start | bytes 24584 | tf_op jit(solution)/shard_map/ppermute | solution.py:28
  36.6 2.7 %copy-start.2 = (s32[8,32,256]{2,1,0:T(8,128)S(1)}, s32[8,32,256]{2,1,0:T(8,128)}, u32[]{:S(2)}) copy-start(s32[8,32,256]{2,1,0:T(8,128)} %param.10) | copy-start | bytes 786436
  36.6 2.7 %copy-start.5 = (f32[8,32,256]{2,1,0:T(8,128)S(1)}, f32[8,32,256]{2,1,0:T(8,128)}, u32[]{:S(2)}) copy-start(f32[8,32,256]{2,1,0:T(8,128)} %param.13) | copy-start | bytes 786436
  37.0 2.3 %collective-permute-start.1 = (f32[1,32,256]{2,1,0:T(8,128)S(1)}, f32[1,32,256]{2,1,0:T(8,128)S(1)}, u32[]{:S(2)}, u32[]{:S(2)}) collective-permute-start(f32[1,32,256]{2,1,0:T(8,128)S(1)} %slice.259), channel_id=1, source_target_pairs={{0,8},{8,16},{16,24},{24,32},{32,40},{40,48},{48,56},{56,64},{64,7... | collective-permute-start | bytes 98312 | tf_op jit(solution)/shard_map/ppermute | solution.py:28
  41.0 8.9 %collective-permute-start.7 = (f32[1,32,256]{2,1,0:T(8,128)S(1)}, f32[1,32,256]{2,1,0:T(8,128)S(1)}, u32[]{:S(2)}, u32[]{:S(2)}) collective-permute-start(f32[1,32,256]{2,1,0:T(8,128)S(1)} %get-tuple-element.36), channel_id=1, source_target_pairs={{0,8},{8,16},{16,24},{24,32},{32,40},{40,48},{48,56},{56,64},{64,7... | collective-permute-start | bytes 98312 | tf_op jit(solution)/shard_map/ppermute | solution.py:19
  48.5 9.0 %collective-permute-start.6 = (f32[1,32,256]{2,1,0:T(8,128)S(1)}, f32[1,32,256]{2,1,0:T(8,128)S(1)}, u32[]{:S(2)}, u32[]{:S(2)}) collective-permute-start(f32[1,32,256]{2,1,0:T(8,128)S(1)} %get-tuple-element.37), channel_id=1, source_target_pairs={{8,0},{16,8},{24,16},{32,24},{40,32},{48,40},{56,48},{64,56},{72,6... | collective-permute-start | bytes 98312 | tf_op jit(solution)/shard_map/ppermute | solution.py:20
  57.6 8.2 %collective-permute-start.9 = (f32[10,1,256]{2,1,0:T(1,128)S(1)}, f32[10,1,256]{2,1,0:T(1,128)S(1)}, u32[]{:S(2)}, u32[]{:S(2)}) collective-permute-start(f32[10,1,256]{2,1,0:T(1,128)S(1)} %get-tuple-element.32), channel_id=1, source_target_pairs={{0,1},{1,2},{2,3},{3,4},{4,5},{5,6},{6,7},{8,9},{9,10},{10,11},{11... | collective-permute-start | bytes 30728 | tf_op jit(solution)/shard_map/ppermute | solution.py:19
  63.9 5.0 %collective-permute-start.8 = (f32[10,1,256]{2,1,0:T(1,128)S(1)}, f32[10,1,256]{2,1,0:T(1,128)S(1)}, u32[]{:S(2)}, u32[]{:S(2)}) collective-permute-start(f32[10,1,256]{2,1,0:T(1,128)S(1)} %get-tuple-element.33), channel_id=1, source_target_pairs={{1,0},{2,1},{3,2},{4,3},{5,4},{6,5},{7,6},{9,8},{10,9},{11,10},{12... | collective-permute-start | bytes 30728 | tf_op jit(solution)/shard_map/ppermute | solution.py:20
  69.5 8.2 %collective-permute-start.11 = (f32[1,32,256]{2,1,0:T(8,128)S(1)}, f32[1,32,256]{2,1,0:T(8,128)S(1)}, u32[]{:S(2)}, u32[]{:S(2)}) collective-permute-start(f32[1,32,256]{2,1,0:T(8,128)S(1)} %get-tuple-element.34), channel_id=1, source_target_pairs={{0,8},{8,16},{16,24},{24,32},{32,40},{40,48},{48,56},{56,64},{64,7... | collective-permute-start | bytes 98312 | tf_op jit(solution)/shard_map/ppermute | solution.py:19
  76.4 8.6 %collective-permute-start.10 = (f32[1,32,256]{2,1,0:T(8,128)S(1)}, f32[1,32,256]{2,1,0:T(8,128)S(1)}, u32[]{:S(2)}, u32[]{:S(2)}) collective-permute-start(f32[1,32,256]{2,1,0:T(8,128)S(1)} %get-tuple-element.35), channel_id=1, source_target_pairs={{8,0},{16,8},{24,16},{32,24},{40,32},{48,40},{56,48},{64,56},{72,6... | collective-permute-start | bytes 98312 | tf_op jit(solution)/shard_map/ppermute | solution.py:20
  85.0 5.7 %collective-permute-start.13 = (f32[10,1,256]{2,1,0:T(1,128)S(1)}, f32[10,1,256]{2,1,0:T(1,128)S(1)}, u32[]{:S(2)}, u32[]{:S(2)}) collective-permute-start(f32[10,1,256]{2,1,0:T(1,128)S(1)} %get-tuple-element.30), channel_id=1, source_target_pairs={{0,1},{1,2},{2,3},{3,4},{4,5},{5,6},{6,7},{8,9},{9,10},{10,11},{11... | collective-permute-start | bytes 30728 | tf_op jit(solution)/shard_map/ppermute | solution.py:19
  88.8 5.0 %collective-permute-start.12 = (f32[10,1,256]{2,1,0:T(1,128)S(1)}, f32[10,1,256]{2,1,0:T(1,128)S(1)}, u32[]{:S(2)}, u32[]{:S(2)}) collective-permute-start(f32[10,1,256]{2,1,0:T(1,128)S(1)} %get-tuple-element.31), channel_id=1, source_target_pairs={{1,0},{2,1},{3,2},{4,3},{5,4},{6,5},{7,6},{9,8},{10,9},{11,10},{12... | collective-permute-start | bytes 30728 | tf_op jit(solution)/shard_map/ppermute | solution.py:20
  94.1 1.1 copy-start.6
where the time goes:
time: 213 us; the launch traced here: 212 us
  blocking collectives  115 us (54%)
  starting transfers between devices  55.6 us (26%)
  waiting for transfers between devices  30.1 us (14%)
  other arithmetic  10.1 us (5%)
    psum x1, blocking collectives, body(): summed = lax.psum(partial_sens, ('len', 'xs'))  115 us
    ppermute x6, starting transfers between devices, with_halo(): before = lax.ppermute(last, axis, up)  34.7 us
    ppermute x6, waiting for transfers between devices, with_halo(): after = lax.ppermute(leading, axis, down)  28.8 us
    ppermute x6, starting transfers between devices, with_halo(): after = lax.ppermute(leading, axis, down)  17.7 us
  transfers between devices with their start and end apart: 14, of which 7 were waited for; matrix products, arithmetic and copies ran while one was open for 1% of the time, Pallas kernels for 0%

commit v1 on v0

v1 whole, which is shorter than its diff:
```python
import math

import jax
import jax.numpy as jnp
from jax import lax
from jax.sharding import Mesh
from jax.sharding import PartitionSpec as P

SWEEPS = 2
PORTS = 16
LEN = ("x", "z", "yh")
XS = ("yl", "c")
SIZES = {"x": 4, "z": 12, "yh": 2, "yl": 4, "c": 2}


def size_of(axes):
    return math.prod(SIZES[a] for a in axes)


def shift(x, axes, by):
    count = size_of(axes)
    pairs = [(i, i + by) for i in range(count) if 0 <= i + by < count]
    return lax.ppermute(x, axes, pairs)


def cut(x, axis, index):
    return lax.slice_in_dim(x, index, index + 1, axis=axis)


def neighbours(x, axis, before, after):
    length = x.shape[axis]
    down = jnp.concatenate([before, lax.slice_in_dim(x, 0, length - 1, axis=axis)], axis=axis)
    up = jnp.concatenate([lax.slice_in_dim(x, 1, length, axis=axis), after], axis=axis)
    return down, up


def edges(x):
    last = [x.shape[0] - 1, x.shape[1] - 1]
    len_before = shift(cut(x, 0, last[0]), LEN, 1)
    len_after = shift(cut(x, 0, 0), LEN, -1)
    xs_before = shift(cut(x, 1, last[1]), XS, 1)
    xs_after = shift(cut(x, 1, 0), XS, -1)
    zero = jnp.zeros_like(cut(x, 2, 0))
    return [(len_before, len_after), (xs_before, xs_after), (zero, zero)]


def total_over(x, axes):
    count = size_of(axes)
    copies = jnp.broadcast_to(x[None], (count,) + x.shape)
    return jnp.sum(lax.all_to_all(copies, axes, 0, 0, tiled=True), axis=0)


def body(alpha, velocity, upwind, celltype, owner, lam_alpha, lam_press):
    opened = (celltype != 1).astype(jnp.float32)
    active = ((celltype == 0) | (celltype == 2)).astype(jnp.float32)
    inlet = (celltype == 2).astype(jnp.float32)
    flows = upwind.astype(jnp.float32)
    rho = 1.0 + 9.0 * alpha
    last = [alpha.shape[0] - 1, alpha.shape[1] - 1]
    passing = 0.4 * velocity * (1.0 - flows)

    def up_message(axis, axes):
        parts = [cut(v, axis, last[axis]) for v in (alpha, lam_alpha, opened, passing[axis])]
        return shift(jnp.concatenate(parts, axis=axis), axes, 1)

    def down_message(axis, axes):
        parts = [cut(v, axis, 0) for v in (alpha, lam_alpha, opened)]
        return shift(jnp.concatenate(parts, axis=axis), axes, -1)

    befores = [up_message(0, LEN), up_message(1, XS), None]
    afters = [down_message(0, LEN), down_message(1, XS), None]
    zero = jnp.zeros_like(cut(alpha, 2, 0))
    befores[2] = jnp.concatenate([zero] * 4, axis=2)
    afters[2] = jnp.concatenate([zero] * 3, axis=2)
    total = lam_alpha
    grads = []
    k_high = []
    k_low = []
    for axis in range(3):
        flow = flows[axis]
        a_b, l_b, o_b, p_b = (cut(befores[axis], axis, i) for i in range(4))
        a_a, l_a, o_a = (cut(afters[axis], axis, i) for i in range(3))
        alpha_prev, alpha_next = neighbours(alpha, axis, a_b, a_a)
        _, lam_next = neighbours(lam_alpha, axis, l_b, l_a)
        open_prev, open_next = neighbours(opened, axis, o_b, o_a)
        face = 0.4 * velocity[axis] * (lam_next - lam_alpha) * (opened * open_next)
        grads.append(face * (flow * alpha + (1.0 - flow) * alpha_next))
        passed = face * (1.0 - flow)
        edge = p_b * (cut(lam_alpha, axis, 0) - l_b) * (o_b * cut(opened, axis, 0))
        incoming, _ = neighbours(passed, axis, edge, zero if axis == 2 else edge)
        total = total + face * flow + incoming
        k_high.append(2.0 * (opened * open_next) / (rho + (1.0 + 9.0 * alpha_next)))
        k_low.append(2.0 * (open_prev * opened) / (1.0 + 9.0 * alpha_prev + rho))
    grad_alpha = opened * total
    grad_velocity = jnp.stack(grads)
    diag = 0.5 + (k_high[0] + k_high[1] + k_high[2]) + (k_low[0] + k_low[1] + k_low[2])
    rhs = lam_press + grad_alpha
    press = active * rhs / diag
    for _ in range(SWEEPS):
        sides = edges(press)
        beside = 0.0
        for axis in range(3):
            down, up = neighbours(press, axis, *sides[axis])
            beside = beside + k_high[axis] * up + k_low[axis] * down
        press = active * (rhs + beside) / diag
    column = jnp.sum((lam_alpha + press) * inlet, axis=0)
    ports = jnp.arange(PORTS, dtype=jnp.int32)
    sens = jnp.sum(jnp.where(owner[None] == ports[:, None, None], column[None], 0.0), axis=(1, 2))
    sens = total_over(sens, ("x", "z"))
    sens = total_over(sens, ("yh", "yl", "c"))
    cells = math.prod(alpha.shape) * size_of(LEN + XS)
    return (grad_alpha, grad_velocity, press, sens / math.sqrt(cells))


def solution(mesh):
    parts = Mesh(mesh.devices.reshape(tuple(SIZES.values())), tuple(SIZES))
    field = P(LEN, XS, None)
    faces = P(None, LEN, XS, None)
    in_specs = (field, faces, faces, field, P(XS, None), field, field)
    out_specs = (field, faces, field, P())
    return jax.shard_map(body, mesh=parts, in_specs=in_specs, out_specs=out_specs, check_vma=False)
```

time: 213 us -> 131 us (0.62)
  blocking collectives: 115 us -> 36.1 us
  local copies, waits for them, and re-layouts: 0.08 us -> 6.9 us
  waiting for transfers between devices: 30.1 us -> 25.6 us
  starting transfers between devices: 55.6 us -> 51.6 us
    psum x1 -> x0, blocking collectives: 115 us -> none  [body(): summed = lax.psum(partial_sens, ('len', 'xs'))]
    all_to_all x0 -> x1, blocking collectives: none -> 36.1 us  [total_over(): return jnp.sum(lax.all_to_all(copies, axes, 0, 0, tiled=True), axis=0)]
    ppermute x14 -> x12, starting transfers between devices: 55.6 us -> 44.5 us  [shift(): return lax.ppermute(x, axes, pairs)]
    ppermute x14 -> x12, waiting for transfers between devices: 30.1 us -> 19.5 us  [shift(): return lax.ppermute(x, axes, pairs)]
    all_to_all x0 -> x1, starting transfers between devices: none -> 7.1 us  [total_over(): return jnp.sum(lax.all_to_all(copies, axes, 0, 0, tiled=True), axis=0)]
    all_to_all x0 -> x1, waiting for transfers between devices: none -> 6.09 us  [total_over(): return jnp.sum(lax.all_to_all(copies, axes, 0, 0, tiled=True), axis=0)]
    slice x5 -> x28, local copies, waits for them, and re-layouts: 0.04 us -> 3.55 us  [the longest x15 2.58 us: cut(): return lax.slice_in_dim(x, index, index + 1, axis=axis)]
    unnamed x14, local copies, waits for them, and re-layouts: 0.04 us -> 2.72 us
  transfers between devices with their start and end apart: 14 -> 13, of which waited for: 7 -> 6; matrix products, arithmetic and copies ran while one was open for 1% -> 2% of each run, Pallas kernels for 0% -> 0%
where the time goes in v1:
time: 131 us; the launch traced here: 130 us
  starting transfers between devices  51.6 us (39%)
  blocking collectives  36.1 us (28%)
  waiting for transfers between devices  25.6 us (20%)
  other arithmetic  8.4 us (6%)
  local copies, waits for them, and re-layouts  6.9 us (5%)
    ppermute x12, starting transfers between devices, shift(): return lax.ppermute(x, axes, pairs)  44.5 us
    all_to_all x1, blocking collectives, total_over(): return jnp.sum(lax.all_to_all(copies, axes, 0, 0, tiled=True), axis=0)  36.1 us
    ppermute x12, waiting for transfers between devices, shift(): return lax.ppermute(x, axes, pairs)  19.5 us
    all_to_all x1, starting transfers between devices, total_over(): return jnp.sum(lax.all_to_all(copies, axes, 0, 0, tiled=True), axis=0)  7.1 us
    all_to_all x1, waiting for transfers between devices, total_over(): return jnp.sum(lax.all_to_all(copies, axes, 0, 0, tiled=True), axis=0)  6.09 us
    unnamed x14, local copies, waits for them, and re-layouts  2.72 us
  transfers between devices with their start and end apart: 13, of which 6 were waited for; matrix products, arithmetic and copies ran while one was open for 2% of the time, Pallas kernels for 0%

profile of v1, /device:TPU:1, one launch (start us, length us, event | category | flops | bytes accessed | tf_op | source)
XLA Modules:
  0.0 129.8 jit_solution(7305406037131996933)
XLA Ops:
  0.6 0.9 slice.262
  1.5 0.9 fusion.67
  2.4 1.0 fusion.50
  3.4 1.5 %subtract_multiply_fusion = f32[3,8,32,256]{3,2,1,0:T(8,128)S(1)} fusion(f32[3,8,32,256]{3,2,1,0:T(8,128)} %param.8, s32[3,8,32,256]{3,2,1,0:T(8,128)} %param.9), kind=kLoop, calls=%fused_computation.1 | loop fusion | flops 786432 | bytes 2359296 | tf_op jit(solution)/shard_map/mul | solution.py:60
  5.0 4.6 %collective-permute-start.3 = (f32[8,4,256]{2,1,0:T(4,128)S(1)}, f32[8,4,256]{2,1,0:T(4,128)S(1)}, u32[]{:S(2)}, u32[]{:S(2)}) collective-permute-start(f32[8,4,256]{2,1,0:T(4,128)S(1)} %pad_maximum_fusion.6), channel_id=1, source_target_pairs={{0,1},{1,2},{2,3},{3,4},{4,5},{5,6},{6,7},{8,9},{9,10},{10,11},{11... | collective-permute-start | bytes 98312 | tf_op jit(solution)/shard_map/ppermute | solution.py:23
  9.7 0.0 slice-start
  9.7 0.7 slice-done
  10.5 6.6 %collective-permute-start.1 = (f32[4,32,256]{2,1,0:T(8,128)S(1)}, f32[4,32,256]{2,1,0:T(8,128)S(1)}, u32[]{:S(2)}, u32[]{:S(2)}) collective-permute-start(f32[4,32,256]{2,1,0:T(8,128)S(1)} %pad_maximum_fusion.3), channel_id=1, source_target_pairs={{0,8},{8,16},{16,24},{24,32},{32,40},{40,48},{48,56},{56,64},{64,7... | collective-permute-start | bytes 393224 | tf_op jit(solution)/shard_map/ppermute | solution.py:23
  17.0 0.2 fusion.64
  17.2 0.1 fusion.66
  17.4 0.1 fusion.61
  17.5 0.1 collective-permute-done.3
  17.5 0.8 copy-done.1
  18.4 3.9 %collective-permute-start.2 = (f32[8,3,256]{2,1,0:T(4,128)S(1)}, f32[8,3,256]{2,1,0:T(4,128)S(1)}, u32[]{:S(2)}, u32[]{:S(2)}) collective-permute-start(f32[8,3,256]{2,1,0:T(4,128)S(1)} %pad_maximum_fusion.5), channel_id=1, source_target_pairs={{1,0},{2,1},{3,2},{4,3},{5,4},{6,5},{7,6},{9,8},{10,9},{11,10},{12... | collective-permute-start | bytes 73736 | tf_op jit(solution)/shard_map/ppermute | solution.py:23
  22.3 0.1 slice.271
  22.4 1.0 copy-done.2
  23.4 0.1 convert_element_type.9
  23.5 0.1 collective-permute-done.2
  23.7 1.3 collective-permute-start
  25.0 0.0 slice-start.1
  25.0 0.2 multiply_bitcast_fusion.1
  25.2 11.2 %collective-permute-done = f32[3,32,256]{2,1,0:T(8,128)S(1)} collective-permute-done((f32[3,32,256]{2,1,0:T(8,128)S(1)}, f32[3,32,256]{2,1,0:T(8,128)S(1)}, u32[]{:S(2)}, u32[]{:S(2)}) %collective-permute-start) | collective-permute-done | bytes 98336 | tf_op jit(solution)/shard_map/ppermute | solution.py:23
  36.4 0.4 multiply_bitcast_fusion.2
  37.0 0.9 copy-done.4
  37.9 0.1 copy-done.5
  38.0 1.7 %fusion.34 = (f32[8,32,256]{2,1,0:T(8,128)S(1)}, f32[8,32,256]{2,1,0:T(8,128)S(1)}, f32[8,32,256]{2,1,0:T(8,128)S(1)}, f32[8,32,256]{2,1,0:T(8,128)S(1)}, f32[8,...) fusion(f32[8,1,256]{2,1,0:T(1,128)S(1)} %get-tuple-element.79, ...), kind=kLoop, calls=%fused_computation.66 | loop fusion | flops 4653056 | bytes 9039872 | tf_op jit(solution)/shard_map/div | solution.py:98
  39.8 0.1 fusion.56
  39.9 5.0 %collective-permute-start.7 = (f32[8,1,256]{2,1,0:T(1,128)S(1)}, f32[8,1,256]{2,1,0:T(1,128)S(1)}, u32[]{:S(2)}, u32[]{:S(2)}) collective-permute-start(f32[8,1,256]{2,1,0:T(1,128)S(1)} %get-tuple-element.41), channel_id=1, source_target_pairs={{0,1},{1,2},{2,3},{3,4},{4,5},{5,6},{6,7},{8,9},{9,10},{10,11},{11... | collective-permute-start | bytes 24584 | tf_op jit(solution)/shard_map/ppermute | solution.py:23
  44.9 1.9 %collective-permute-start.6 = (f32[8,1,256]{2,1,0:T(1,128)S(1)}, f32[8,1,256]{2,1,0:T(1,128)S(1)}, u32[]{:S(2)}, u32[]{:S(2)}) collective-permute-start(f32[8,1,256]{2,1,0:T(1,128)S(1)} %get-tuple-element.42), channel_id=1, source_target_pairs={{1,0},{2,1},{3,2},{4,3},{5,4},{6,5},{7,6},{9,8},{10,9},{11,10},{12... | collective-permute-start | bytes 24584 | tf_op jit(solution)/shard_map/ppermute | solution.py:23
  46.9 3.7 %collective-permute-start.5 = (f32[1,32,256]{2,1,0:T(8,128)S(1)}, f32[1,32,256]{2,1,0:T(8,128)S(1)}, u32[]{:S(2)}, u32[]{:S(2)}) collective-permute-start(f32[1,32,256]{2,1,0:T(8,128)S(1)} %get-tuple-element.45), channel_id=1, source_target_pairs={{0,8},{8,16},{16,24},{24,32},{32,40},{40,48},{48,56},{56,64},{64,7... | collective-permute-start | bytes 98312 | tf_op jit(solution)/shard_map/ppermute | solution.py:23
  50.6 1.3 collective-permute-start.4
  51.9 7.2 %collective-permute-done.4 = f32[1,32,256]{2,1,0:T(8,128)S(1)} collective-permute-done((f32[1,32,256]{2,1,0:T(8,128)S(1)}, f32[1,32,256]{2,1,0:T(8,128)S(1)}, u32[]{:S(2)}, u32[]{:S(2)}) %collective-permute-start.4) | collective-permute-done | bytes 32800 | tf_op jit(solution)/shard_map/ppermute | solution.py:23
  59.1 0.4 fusion.24
  59.6 0.1 fusion.55
  59.8 1.9 %collective-permute-start.10 = (f32[8,1,256]{2,1,0:T(1,128)S(1)}, f32[8,1,256]{2,1,0:T(1,128)S(1)}, u32[]{:S(2)}, u32[]{:S(2)}) collective-permute-start(f32[8,1,256]{2,1,0:T(1,128)S(1)} %get-tuple-element.35), channel_id=1, source_target_pairs={{1,0},{2,1},{3,2},{4,3},{5,4},{6,5},{7,6},{9,8},{10,9},{11,10},{12... | collective-permute-start | bytes 24584 | tf_op jit(solution)/shard_map/ppermute | solution.py:23
  61.7 5.2 %collective-permute-start.11 = (f32[8,1,256]{2,1,0:T(1,128)S(1)}, f32[8,1,256]{2,1,0:T(1,128)S(1)}, u32[]{:S(2)}, u32[]{:S(2)}) collective-permute-start(f32[8,1,256]{2,1,0:T(1,128)S(1)} %get-tuple-element.36), channel_id=1, source_target_pairs={{0,1},{1,2},{2,3},{3,4},{4,5},{5,6},{6,7},{8,9},{9,10},{10,11},{11... | collective-permute-start | bytes 24584 | tf_op jit(solution)/shard_map/ppermute | solution.py:23
  66.8 1.3 collective-permute-start.8
  68.1 7.9 %collective-permute-start.9 = (f32[1,32,256]{2,1,0:T(8,128)S(1)}, f32[1,32,256]{2,1,0:T(8,128)S(1)}, u32[]{:S(2)}, u32[]{:S(2)}) collective-permute-start(f32[1,32,256]{2,1,0:T(8,128)S(1)} %get-tuple-element.32), channel_id=1, source_target_pairs={{0,8},{8,16},{16,24},{24,32},{32,40},{40,48},{48,56},{56,64},{64,7... | collective-permute-start | bytes 98312 | tf_op jit(solution)/shard_map/ppermute | solution.py:23
  76.1 0.9 collective-permute-done.9
  77.1 1.0 select_reduce_fusion.1
  78.1 0.2 select_reduce_fusion
  78.3 36.1 %all_to_all.12 = f32[48,1,16]{2,1,0:T(1,128)S(1)} all-to-all(f32[48,1,16]{2,1,0:T(1,128)S(1)} %broadcast_in_dim.18), channel_id=1, replica_groups=mesh['x'=4,'z'=12,'yh'=2,'yl'=4,'c'=2] {'x','z'}, dimensions={0} | all-to-all | bytes 6144 | tf_op jit(solution)/shard_map/all_to_all | solution.py:50
  114.5 0.1 reduce_sum.38
  114.5 0.6 broadcast_in_dim.30
  115.1 7.1 %all-to-all-start.1 = ((f32[16,1,16]{2,1,0:T(1,128)}), f32[16,1,16]{2,1,0:T(1,128)S(1)}, u32[]{:S(2)}, u32[]{:S(2)}) async-start(f32[16,1,16]{2,1,0:T(1,128)} %broadcast_in_dim.30), calls=%async_computation.1 | async-start | bytes 16384 | tf_op jit(solution)/shard_map/all_to_all | solution.py:50
  122.2 0.9 pad_maximum_fusion
  123.2 6.1 %all-to-all-done.1 = f32[16,1,16]{2,1,0:T(1,128)S(1)} async-done(((f32[16,1,16]{2,1,0:T(1,128)}), f32[16,1,16]{2,1,0:T(1,128)S(1)}, u32[]{:S(2)}, u32[]{:S(2)}) %all-to-all-start.1) | async-done | bytes 1056 | tf_op jit(solution)/shard_map/all_to_all | solution.py:50
  129.3 0.5 broadcast_multiply_fusion
  (47 shorter events, 0.7 us)
Async XLA Ops:
  4.9 4.7 %copy-start = (f32[8,32,256]{2,1,0:T(8,128)S(1)}, f32[8,32,256]{2,1,0:T(8,128)}, u32[]{:S(2)}) copy-start(f32[8,32,256]{2,1,0:T(8,128)} %param.7) | copy-start | bytes 786436
  5.0 12.5 %collective-permute-start.3 = (f32[8,4,256]{2,1,0:T(4,128)S(1)}, f32[8,4,256]{2,1,0:T(4,128)S(1)}, u32[]{:S(2)}, u32[]{:S(2)}) collective-permute-start(f32[8,4,256]{2,1,0:T(4,128)S(1)} %pad_maximum_fusion.6), channel_id=1, source_target_pairs={{0,1},{1,2},{2,3},{3,4},{4,5},{5,6},{6,7},{8,9},{9,10},{10,11},{11... | collective-permute-start | bytes 98312 | tf_op jit(solution)/shard_map/ppermute | solution.py:23
  9.7 0.8 slice-start
  10.5 13.2 %collective-permute-start.1 = (f32[4,32,256]{2,1,0:T(8,128)S(1)}, f32[4,32,256]{2,1,0:T(8,128)S(1)}, u32[]{:S(2)}, u32[]{:S(2)}) collective-permute-start(f32[4,32,256]{2,1,0:T(8,128)S(1)} %pad_maximum_fusion.3), channel_id=1, source_target_pairs={{0,8},{8,16},{16,24},{24,32},{32,40},{40,48},{48,56},{56,64},{64,7... | collective-permute-start | bytes 393224 | tf_op jit(solution)/shard_map/ppermute | solution.py:23
  17.3 1.0 copy-start.1
  18.4 5.2 %collective-permute-start.2 = (f32[8,3,256]{2,1,0:T(4,128)S(1)}, f32[8,3,256]{2,1,0:T(4,128)S(1)}, u32[]{:S(2)}, u32[]{:S(2)}) collective-permute-start(f32[8,3,256]{2,1,0:T(4,128)S(1)} %pad_maximum_fusion.5), channel_id=1, source_target_pairs={{1,0},{2,1},{3,2},{4,3},{5,4},{6,5},{7,6},{9,8},{10,9},{11,10},{12... | collective-permute-start | bytes 73736 | tf_op jit(solution)/shard_map/ppermute | solution.py:23
  22.3 1.1 copy-start.2
  23.4 1.6 %copy-start.3 = (f32[3,8,32,256]{3,2,1,0:T(8,128)S(1)}, f32[3,8,32,256]{3,2,1,0:T(8,128)}, u32[]{:S(2)}) copy-start(f32[3,8,32,256]{3,2,1,0:T(8,128)} %param.8) | copy-start | bytes 2359300
  23.7 12.7 %collective-permute-start = (f32[3,32,256]{2,1,0:T(8,128)S(1)}, f32[3,32,256]{2,1,0:T(8,128)S(1)}, u32[]{:S(2)}, u32[]{:S(2)}) collective-permute-start(f32[3,32,256]{2,1,0:T(8,128)S(1)} %pad_maximum_fusion.4), channel_id=1, source_target_pairs={{8,0},{16,8},{24,16},{32,24},{40,32},{48,40},{56,48},{64,56},{72,6... | collective-permute-start | bytes 294920 | tf_op jit(solution)/shard_map/ppermute | solution.py:23
  25.0 11.4 %slice-start.1 = ((f32[8,32,256]{2,1,0:T(8,128)}), f32[7,32,256]{2,1,0:T(8,128)S(1)}, s32[]{:S(2)}) async-start(f32[8,32,256]{2,1,0:T(8,128)} %param.12), calls=%async_computation.3 | async-start | bytes 458752 | tf_op jit(solution)/shard_map/slice | solution.py:33
  36.9 1.0 copy-start.4
  37.0 1.0 copy-start.5
  39.9 12.0 %collective-permute-start.7 = (f32[8,1,256]{2,1,0:T(1,128)S(1)}, f32[8,1,256]{2,1,0:T(1,128)S(1)}, u32[]{:S(2)}, u32[]{:S(2)}) collective-permute-start(f32[8,1,256]{2,1,0:T(1,128)S(1)} %get-tuple-element.41), channel_id=1, source_target_pairs={{0,1},{1,2},{2,3},{3,4},{4,5},{5,6},{6,7},{8,9},{9,10},{10,11},{11... | collective-permute-start | bytes 24584 | tf_op jit(solution)/shard_map/ppermute | solution.py:23
  44.9 7.0 %collective-permute-start.6 = (f32[8,1,256]{2,1,0:T(1,128)S(1)}, f32[8,1,256]{2,1,0:T(1,128)S(1)}, u32[]{:S(2)}, u32[]{:S(2)}) collective-permute-start(f32[8,1,256]{2,1,0:T(1,128)S(1)} %get-tuple-element.42), channel_id=1, source_target_pairs={{1,0},{2,1},{3,2},{4,3},{5,4},{6,5},{7,6},{9,8},{10,9},{11,10},{12... | collective-permute-start | bytes 24584 | tf_op jit(solution)/shard_map/ppermute | solution.py:23
  46.9 5.1 %collective-permute-start.5 = (f32[1,32,256]{2,1,0:T(8,128)S(1)}, f32[1,32,256]{2,1,0:T(8,128)S(1)}, u32[]{:S(2)}, u32[]{:S(2)}) collective-permute-start(f32[1,32,256]{2,1,0:T(8,128)S(1)} %get-tuple-element.45), channel_id=1, source_target_pairs={{0,8},{8,16},{16,24},{24,32},{32,40},{40,48},{48,56},{56,64},{64,7... | collective-permute-start | bytes 98312 | tf_op jit(solution)/shard_map/ppermute | solution.py:23
  50.6 8.6 %collective-permute-start.4 = (f32[1,32,256]{2,1,0:T(8,128)S(1)}, f32[1,32,256]{2,1,0:T(8,128)S(1)}, u32[]{:S(2)}, u32[]{:S(2)}) collective-permute-start(f32[1,32,256]{2,1,0:T(8,128)S(1)} %get-tuple-element.46), channel_id=1, source_target_pairs={{8,0},{16,8},{24,16},{32,24},{40,32},{48,40},{56,48},{64,56},{72,6... | collective-permute-start | bytes 98312 | tf_op jit(solution)/shard_map/ppermute | solution.py:23
  59.8 16.3 %collective-permute-start.10 = (f32[8,1,256]{2,1,0:T(1,128)S(1)}, f32[8,1,256]{2,1,0:T(1,128)S(1)}, u32[]{:S(2)}, u32[]{:S(2)}) collective-permute-start(f32[8,1,256]{2,1,0:T(1,128)S(1)} %get-tuple-element.35), channel_id=1, source_target_pairs={{1,0},{2,1},{3,2},{4,3},{5,4},{6,5},{7,6},{9,8},{10,9},{11,10},{12... | collective-permute-start | bytes 24584 | tf_op jit(solution)/shard_map/ppermute | solution.py:23
  61.7 14.4 %collective-permute-start.11 = (f32[8,1,256]{2,1,0:T(1,128)S(1)}, f32[8,1,256]{2,1,0:T(1,128)S(1)}, u32[]{:S(2)}, u32[]{:S(2)}) collective-permute-start(f32[8,1,256]{2,1,0:T(1,128)S(1)} %get-tuple-element.36), channel_id=1, source_target_pairs={{0,1},{1,2},{2,3},{3,4},{4,5},{5,6},{6,7},{8,9},{9,10},{10,11},{11... | collective-permute-start | bytes 24584 | tf_op jit(solution)/shard_map/ppermute | solution.py:23
  66.8 9.3 %collective-permute-start.8 = (f32[1,32,256]{2,1,0:T(8,128)S(1)}, f32[1,32,256]{2,1,0:T(8,128)S(1)}, u32[]{:S(2)}, u32[]{:S(2)}) collective-permute-start(f32[1,32,256]{2,1,0:T(8,128)S(1)} %get-tuple-element.31), channel_id=1, source_target_pairs={{8,0},{16,8},{24,16},{32,24},{40,32},{48,40},{56,48},{64,56},{72,6... | collective-permute-start | bytes 98312 | tf_op jit(solution)/shard_map/ppermute | solution.py:23
  68.1 8.9 %collective-permute-start.9 = (f32[1,32,256]{2,1,0:T(8,128)S(1)}, f32[1,32,256]{2,1,0:T(8,128)S(1)}, u32[]{:S(2)}, u32[]{:S(2)}) collective-permute-start(f32[1,32,256]{2,1,0:T(8,128)S(1)} %get-tuple-element.32), channel_id=1, source_target_pairs={{0,8},{8,16},{16,24},{24,32},{32,40},{40,48},{48,56},{56,64},{64,7... | collective-permute-start | bytes 98312 | tf_op jit(solution)/shard_map/ppermute | solution.py:23
  77.0 1.1 copy-start.6
  115.1 14.1 %all-to-all-start.1 = ((f32[16,1,16]{2,1,0:T(1,128)}), f32[16,1,16]{2,1,0:T(1,128)S(1)}, u32[]{:S(2)}, u32[]{:S(2)}) async-start(f32[16,1,16]{2,1,0:T(1,128)} %broadcast_in_dim.30), calls=%async_computation.1 | async-start | bytes 16384 | tf_op jit(solution)/shard_map/all_to_all | solution.py:50

commit v2 on v1

v2 whole, which is shorter than its diff:
```python
import functools
import math

import jax
import jax.numpy as jnp
from jax import lax
from jax.experimental import pallas as pl
from jax.experimental.pallas import tpu as pltpu
from jax.sharding import Mesh
from jax.sharding import PartitionSpec as P

SWEEPS = 2
PORTS = 16
LEN = ("x", "z", "yh")
XS = ("yl", "c")
FIRST = ("x", "yh", "yl")
SECOND = ("z", "c")
SIZES = {"x": 4, "z": 12, "yh": 2, "yl": 4, "c": 2}
PLANES = 8
ROWS = 32
HALO = 8
EXT = ROWS + HALO
NZ = 256
WALL = 1e30
STRIP = (("t", 3), ("al", 3), ("la", 3), ("lp", 2), ("c0", 2), ("m0", 2), ("c1", 3), ("m1", 2), ("c2", 2), ("m2", 2))
FIELDS = [name for name, _ in STRIP]
DOWN_ROWS = 6 * ROWS + 2 * HALO
UP_ROWS = 8 * ROWS + 3 * HALO


def size_of(axes):
    return math.prod(SIZES[a] for a in axes)


def shift(x, axes, by):
    count = size_of(axes)
    pairs = [(i, i + by) for i in range(count) if 0 <= i + by < count]
    return lax.ppermute(x, axes, pairs)


def up_y(x):
    return pltpu.roll(x, EXT - 1, 0)


def down_y(x):
    return pltpu.roll(x, 1, 0)


def up_z(x):
    return pltpu.roll(x, NZ - 1, 1)


def down_z(x):
    return pltpu.roll(x, 1, 1)


def resistance(t, alpha):
    return jnp.where(t != 0.0, 1.0 + 9.0 * alpha, WALL)


def coupling(low, high):
    both = low + high
    through = both < 0.5 * WALL
    return through, jnp.where(through, 2.0 / both, 0.0)


def is_active(t):
    return jnp.abs(t) == 1.0


def split_flux(through, speed, donor, low, high):
    face = jnp.where(through, speed * (high - low), 0.0)
    stays = face * donor
    return stays, face - stays


def lanes(shape):
    return lax.broadcasted_iota(jnp.int32, shape, 1)


def sublanes(shape):
    return lax.broadcasted_iota(jnp.int32, shape, 0)


def strip_kernel(al_l, ve_l, up_l, ct_l, la_l, lp_l, al_f, ve_f, up_f, ct_f, la_f, lp_f, to_next, to_prev):
    for out, al, ve, up, ct, la, lp, last in (
        (to_next, al_l, ve_l, up_l, ct_l, la_l, lp_l, True),
        (to_prev, al_f, ve_f, up_f, ct_f, la_f, lp_f, False),
    ):
        at = 0
        for name, count in STRIP:
            first = HALO - count if last else 0
            rows = pl.ds(first, count)
            if name == "t":
                value = ct[:, rows, :].astype(jnp.float32) - 1.0
            elif name == "al":
                value = al[:, rows, :]
            elif name == "la":
                value = la[:, rows, :]
            elif name == "lp":
                value = lp[:, rows, :]
            elif name[0] == "c":
                value = 0.4 * ve[int(name[1]), :, rows, :]
                if name == "c1" and last:
                    donor = up[1, :, rows, :].astype(jnp.float32)
                    row = lax.broadcasted_iota(jnp.int32, value.shape, 1)
                    value = jnp.where(row == 0, value * (1.0 - donor), value)
            else:
                value = up[int(name[1]), :, rows, :].astype(jnp.float32)
            out[:, pl.ds(at, count), :] = value
            at += count


def strips(alpha, velocity, upwind, celltype, lam, lam_press):
    def block(x, last):
        index = x.shape[-2] // HALO - 1 if last else 0
        if x.ndim == 3:
            return pl.BlockSpec((PLANES, HALO, NZ), lambda i: (0, index, 0))
        return pl.BlockSpec((3, PLANES, HALO, NZ), lambda i: (0, 0, index, 0))

    args = (alpha, velocity, upwind, celltype, lam, lam_press)
    message = jax.ShapeDtypeStruct((PLANES, 24, NZ), jnp.float32)
    whole = pl.BlockSpec((PLANES, 24, NZ), lambda i: (0, 0, 0))
    return pl.pallas_call(
        strip_kernel,
        grid=(1,),
        in_specs=[block(x, True) for x in args] + [block(x, False) for x in args],
        out_specs=[whole, whole],
        out_shape=[message, message],
        name="strips",
    )(*args, *args)


class Own:
    def __init__(self, al, ve, up, ct, la, lp, halo):
        self.refs = (al, ve, up, ct, la, lp, halo)

    def get(self, name, p):
        al, ve, up, ct, la, lp, halo = self.refs
        if name == "t":
            own = ct[p].astype(jnp.float32) - 1.0
        elif name in ("al", "la", "lp"):
            own = {"al": al, "la": la, "lp": lp}[name][p]
        elif name[0] == "c":
            own = 0.4 * ve[int(name[1]), p]
        else:
            own = up[int(name[1]), p].astype(jnp.float32)
        return jnp.concatenate([own, halo[FIELDS.index(name), p]], axis=0)

    def resist(self, p):
        return resistance(self.get("t", p), self.get("al", p))


def in_plane(r):
    through_y, ky = coupling(r, up_y(r))
    through_z, kz = coupling(r, up_z(r))
    inside = lanes(r.shape) < NZ - 1
    return through_y, ky, through_z & inside, jnp.where(inside, kz, 0.0)


def in_plane_terms(own, p, r):
    through_y, ky, through_z, kz = in_plane(r)
    la = own.get("la", p)
    stays, passes = split_flux(through_y, own.get("c1", p), own.get("m1", p), la, up_y(la))
    flux = stays + down_y(passes)
    stays, passes = split_flux(through_z, own.get("c2", p), own.get("m2", p), la, up_z(la))
    flux = flux + (stays + down_z(passes))
    return flux, ky + down_y(ky), kz + down_z(kz), ky, kz


def between(own, p):
    through, k = coupling(own.resist(p), own.resist(p + 1))
    stays, passes = split_flux(through, own.get("c0", p), own.get("m0", p), own.get("la", p), own.get("la", p + 1))
    return k, stays, passes


def fill_halo(prev, nxt, halo):
    at = 0
    halo[...] = jnp.zeros(halo.shape, jnp.float32)
    for f, (_, count) in enumerate(STRIP):
        halo[f, :, pl.ds(0, count), :] = nxt[:, pl.ds(at, count), :]
        halo[f, :, pl.ds(HALO - count, count), :] = prev[:, pl.ds(at, count), :]
        at += count


def pack_pair(a, b):
    row = sublanes(a.shape)
    low = (row == 2) | (row == 3)
    high = (row == 4) | (row == 5)
    return jnp.where(low, pltpu.roll(b, 2, 0), jnp.where(high, pltpu.roll(b, HALO - 2, 0), a))


def pack_trio(a, b, c):
    row = sublanes(a.shape)
    out = jnp.where(row == 2, pltpu.roll(b, 2, 0), a)
    out = jnp.where(row == 5, pltpu.roll(b, HALO - 2, 0), out)
    out = jnp.where(row == 3, pltpu.roll(c, 3, 0), out)
    return jnp.where(row == 4, pltpu.roll(c, HALO - 3, 0), out)


def outer(a):
    row = sublanes(a.shape)
    return jnp.where((row < 2) | (row > 5), a, 0.0)


def unpack_pair(tile):
    row = sublanes(tile.shape)
    b = jnp.where(row < 2, pltpu.roll(tile, HALO - 2, 0), jnp.where(row > 5, pltpu.roll(tile, 2, 0), 0.0))
    return outer(tile), b


def unpack_trio(tile):
    row = sublanes(tile.shape)
    b = jnp.where(row == 0, pltpu.roll(tile, HALO - 2, 0), jnp.where(row == 7, pltpu.roll(tile, 2, 0), 0.0))
    c = jnp.where(row == 0, pltpu.roll(tile, HALO - 3, 0), jnp.where(row == 7, pltpu.roll(tile, 3, 0), 0.0))
    return outer(tile), b, c


def slab_kernel(al, ve, up, ct, la, lp, prev, nxt, halo, down, upper):
    fill_halo(prev, nxt, halo)
    own = Own(al, ve, up, ct, la, lp, halo)
    top = PLANES - 1
    for out, edge, inner, far in ((down, 0, 1, 2), (upper, top, top - 1, top - 2)):
        low, lower_far = (edge, inner) if edge == 0 else (inner, far)
        k_edge, stays_edge, passes_edge = between(own, low)
        k_far, stays_far, passes_far = between(own, lower_far)
        if edge == 0:
            edge_flux, inner_flux = stays_edge, passes_edge + stays_far
        else:
            edge_flux, inner_flux = passes_edge, stays_edge + passes_far

        def sums(p, flux_len, k_len):
            flux, sum_y, sum_z, _, _ = in_plane_terms(own, p, own.resist(p))
            t = own.get("t", p)
            source = own.get("lp", p) + jnp.where(t != 0.0, own.get("la", p) + (flux_len + flux), 0.0)
            return t, source, 0.5 + (k_len + sum_y + sum_z)

        t_in, source_in, diag_in = sums(inner, inner_flux, k_edge + k_far)
        carried = k_edge * jnp.where(is_active(t_in), source_in / diag_in, 0.0)
        t, source, diag = sums(edge, edge_flux, k_edge)
        alpha, lam = own.get("al", edge), own.get("la", edge)
        planes = [t, alpha, lam, source, diag, carried]
        tiles = [pack_pair(t[ROWS:], alpha[ROWS:]), pack_trio(lam[ROWS:], source[ROWS:], diag[ROWS:])]
        if edge != 0:
            speed, donor = own.get("c0", edge), own.get("m0", edge)
            planes += [speed, donor]
            tiles.append(pack_pair(speed[ROWS:], donor[ROWS:]))
        for i, plane in enumerate(planes):
            out[pl.ds(i * ROWS, ROWS), :] = plane[:ROWS]
        for i, tile in enumerate(tiles):
            out[pl.ds(len(planes) * ROWS + i * HALO, HALO), :] = tile


def slabs(alpha, velocity, upwind, celltype, lam, lam_press, prev, nxt):
    return pl.pallas_call(
        slab_kernel,
        out_shape=[
            jax.ShapeDtypeStruct((len(FIELDS), PLANES, HALO, NZ), jnp.float32),
            jax.ShapeDtypeStruct((DOWN_ROWS, NZ), jnp.float32),
            jax.ShapeDtypeStruct((UP_ROWS, NZ), jnp.float32),
        ],
        name="slabs",
    )(alpha, velocity, upwind, celltype, lam, lam_press, prev, nxt)


def read_message(ref, with_faces):
    count = 8 if with_faces else 6
    planes = [ref[pl.ds(i * ROWS, ROWS), :] for i in range(count)]
    tiles = [ref[pl.ds(count * ROWS + i * HALO, HALO), :] for i in range(count // 2 - 1)]
    t, alpha = unpack_pair(tiles[0])
    lam, source, diag = unpack_trio(tiles[1])
    halos = [t, alpha, lam, source, diag, jnp.zeros_like(t)]
    if with_faces:
        halos += list(unpack_pair(tiles[2]))
    return [jnp.concatenate([a, b], axis=0) for a, b in zip(planes, halos)]


def relax_kernel(
    al, ve, up, ct, la, lp, ow, halo, below, above, grad, press, sums, kl, ky, kz, source, scale, first, second
):
    own = Own(al, ve, up, ct, la, lp, halo)
    t_b, al_b, la_b, src_b, diag_b, carried_b, c_b, m_b = read_message(below, True)
    t_a, al_a, la_a, src_a, diag_a, carried_a = read_message(above, False)
    r_b, r_a = resistance(t_b, al_b), resistance(t_a, al_a)
    top = PLANES - 1

    def weight(t, diag):
        return jnp.where(is_active(t) & (diag >= 0.5), 1.0 / diag, 0.0)

    through, k = coupling(r_b, own.resist(0))
    stays, passes = split_flux(through, c_b, m_b, la_b, own.get("la", 0))
    kl[0] = k
    _, ky[0], _, kz[0] = in_plane(r_b)
    source[0] = src_b + stays
    scale[0] = weight(t_b, diag_b + k)
    first[0] = source[0] * scale[0]
    source[0] = source[0] + carried_b
    incoming = passes
    for p in range(PLANES):
        r = own.resist(p)
        lam = own.get("la", p)
        r_next = own.resist(p + 1) if p < top else r_a
        lam_next = own.get("la", p + 1) if p < top else la_a
        through, k = coupling(r, r_next)
        stays, passes = split_flux(through, own.get("c0", p), own.get("m0", p), lam, lam_next)
        flux, sum_y, sum_z, k_y, k_z = in_plane_terms(own, p, r)
        t = own.get("t", p)
        total = jnp.where(t != 0.0, lam + ((incoming + stays) + flux), 0.0)
        grad[p] = total[:ROWS]
        kl[p + 1], ky[p + 1], kz[p + 1] = k, k_y, k_z
        source[p + 1] = own.get("lp", p) + total
        scale[p + 1] = weight(t, 0.5 + ((k + kl[p]) + sum_y + sum_z))
        first[p + 1] = source[p + 1] * scale[p + 1]
        incoming = passes
    k = kl[PLANES]
    _, ky[PLANES + 1], _, kz[PLANES + 1] = in_plane(r_a)
    source[PLANES + 1] = src_a + incoming
    scale[PLANES + 1] = weight(t_a, diag_a + k)
    first[PLANES + 1] = source[PLANES + 1] * scale[PLANES + 1]
    source[PLANES + 1] = source[PLANES + 1] + carried_a

    def sweep(x, i):
        mid = x[i]
        k_y, k_z = ky[i], kz[i]
        beside = k_y * up_y(mid) + down_y(k_y) * down_y(mid)
        beside = beside + (k_z * up_z(mid) + down_z(k_z) * down_z(mid))
        if i <= PLANES:
            beside = beside + kl[i] * x[i + 1]
        if i > 0:
            beside = beside + kl[i - 1] * x[i - 1]
        return (source[i] + beside) * scale[i]

    for i in range(PLANES + 2):
        second[i] = sweep(first, i)
    column = jnp.zeros((ROWS, NZ), jnp.float32)
    for p in range(PLANES):
        x = sweep(second, p + 1)[:ROWS]
        press[p] = x
        column = column + jnp.where(ct[p] == 2, la[p] + x, 0.0)
    owner = ow[...]
    parts = []
    for port in range(PORTS):
        mine = jnp.where(owner == port, column, 0.0)
        mine = mine[:, :128] + mine[:, 128:]
        parts.append(jnp.sum(mine, axis=0, keepdims=True))
    table = jnp.sum(jnp.concatenate(parts, axis=0), axis=1, keepdims=True)
    diagonal = lanes((PORTS, 128)) == sublanes((PORTS, 128))
    line = jnp.sum(jnp.where(diagonal, table, 0.0), axis=0, keepdims=True)
    sums[...] = jnp.broadcast_to(line, sums.shape)


def relax(alpha, velocity, upwind, celltype, lam, lam_press, owner, halo, below, above):
    plane = functools.partial(pltpu.VMEM, dtype=jnp.float32)
    field = jax.ShapeDtypeStruct((PLANES, ROWS, NZ), jnp.float32)
    return pl.pallas_call(
        relax_kernel,
        out_shape=[field, field, jax.ShapeDtypeStruct((size_of(FIRST), 128), jnp.float32)],
        scratch_shapes=[plane((PLANES + 2, EXT, NZ)) for _ in range(7)],
        name="relax",
    )(alpha, velocity, upwind, celltype, lam, lam_press, owner, halo, below, above)


def faces_kernel(al, ve, up, ct, la, lp, halo, above, out):
    own = Own(al, ve, up, ct, la, lp, halo)
    t_a, al_a, la_a = read_message(above, False)[:3]
    r_a = resistance(t_a, al_a)

    def write(axis, p, through, speed, donor, lam, lam_next, alpha, alpha_next):
        face = jnp.where(through, speed * (lam_next - lam), 0.0)
        out[axis, p] = (face * jnp.where(donor != 0.0, alpha, alpha_next))[:ROWS]

    for p in range(PLANES):
        r, alpha, lam = own.resist(p), own.get("al", p), own.get("la", p)
        inner = p < PLANES - 1
        r_next = own.resist(p + 1) if inner else r_a
        alpha_next = own.get("al", p + 1) if inner else al_a
        lam_next = own.get("la", p + 1) if inner else la_a
        through, _ = coupling(r, r_next)
        write(0, p, through, own.get("c0", p), own.get("m0", p), lam, lam_next, alpha, alpha_next)
        through, _ = coupling(r, up_y(r))
        write(1, p, through, own.get("c1", p), own.get("m1", p), lam, up_y(lam), alpha, up_y(alpha))
        through, _ = coupling(r, up_z(r))
        through = through & (lanes(r.shape) < NZ - 1)
        write(2, p, through, own.get("c2", p), own.get("m2", p), lam, up_z(lam), alpha, up_z(alpha))


def faces(alpha, velocity, upwind, celltype, lam, lam_press, halo, above):
    return pl.pallas_call(
        faces_kernel,
        out_shape=jax.ShapeDtypeStruct((3, PLANES, ROWS, NZ), jnp.float32),
        name="faces",
    )(alpha, velocity, upwind, celltype, lam, lam_press, halo, above)


def total_over(copies, axes):
    return jnp.sum(lax.all_to_all(copies, axes, 0, 0, tiled=True), axis=0)


def body(alpha, velocity, upwind, celltype, owner, lam_alpha, lam_press):
    args = (alpha, velocity, upwind, celltype, lam_alpha, lam_press)
    to_next, to_prev = strips(*args)
    prev = shift(to_next, XS, 1)
    nxt = shift(to_prev, XS, -1)
    halo, down, upper = slabs(*args, prev, nxt)
    below = shift(upper, LEN, 1)
    above = shift(down, LEN, -1)
    grad_alpha, press, sums = relax(*args, owner, halo, below, above)
    grad_velocity = faces(*args, halo, above)
    sums = total_over(sums, FIRST)
    sums = total_over(jnp.broadcast_to(sums[None], (size_of(SECOND), 128)), SECOND)
    cells = math.prod(alpha.shape) * size_of(LEN + XS)
    return (grad_alpha, grad_velocity, press, sums[:PORTS] / math.sqrt(cells))


def solution(mesh):
    parts = Mesh(mesh.devices.reshape(tuple(SIZES.values())), tuple(SIZES))
    field = P(LEN, XS, None)
    faces_spec = P(None, LEN, XS, None)
    in_specs = (field, faces_spec, faces_spec, field, P(XS, None), field, field)
    out_specs = (field, faces_spec, field, P())
    return jax.shard_map(body, mesh=parts, in_specs=in_specs, out_specs=out_specs, check_vma=False)
```

time: 131 us -> 97.2 us (0.74)
  blocking collectives: 36.1 us -> 13.7 us
  starting transfers between devices: 51.6 us -> 31.9 us
  Pallas kernels: 0 us -> 13.4 us
  waiting for transfers between devices: 25.6 us -> 34.4 us
  other arithmetic: 8.4 us -> 0.58 us
  local copies, waits for them, and re-layouts: 6.9 us -> 2.06 us
    ppermute x12 -> x4, starting transfers between devices: 44.5 us -> 18.4 us  [shift(): return lax.ppermute(x, axes, pairs)]
    all_to_all x1, blocking collectives: 36.1 us -> 13.7 us  [total_over(): return jnp.sum(lax.all_to_all(copies, axes, 0, 0, tiled=True), axis=0)]
    pallas_call x0 -> x4, Pallas kernels: none -> 13.4 us  [the longest x1 4.55 us: relax(): pl.pallas_call(relax_kernel, out_shape=[field, field, jax.ShapeDtypeStruc...]
    ppermute x12 -> x4, waiting for transfers between devices: 19.5 us -> 28.3 us  [shift(): return lax.ppermute(x, axes, pairs)]
    all_to_all x1, starting transfers between devices: 7.1 us -> 13.6 us  [total_over(): return jnp.sum(lax.all_to_all(copies, axes, 0, 0, tiled=True), axis=0)]
    slice x28 -> x0, local copies, waits for them, and re-layouts: 3.55 us -> none  [the longest x15 2.58 us: cut(): return lax.slice_in_dim(x, index, index + 1, axis=axis)]
    div x3 -> x1, other arithmetic: 2.61 us -> 0.52 us  [body(): return (grad_alpha, grad_velocity, press, sums[:PORTS] / math.sqrt(cells))]
    mul x7 -> x0, other arithmetic: 1.73 us -> none  [the longest x1 1.54 us: body(): passing = 0.4 * velocity * (1.0 - flows)]
  transfers between devices with their start and end apart: 13 -> 5, of which waited for: 6 -> 3; matrix products, arithmetic and copies ran while one was open for 2% -> 0% of each run, Pallas kernels for 0% -> 3%
where the time goes in v2:
time: 97.2 us; the launch traced here: 96.8 us
  waiting for transfers between devices  34.4 us (35%)
  starting transfers between devices  31.9 us (33%)
  blocking collectives  13.7 us (14%)
  Pallas kernels  13.4 us (14%)
  local copies, waits for them, and re-layouts  2.06 us (2%)
    ppermute x4, waiting for transfers between devices, shift(): return lax.ppermute(x, axes, pairs)  28.3 us
    ppermute x4, starting transfers between devices, shift(): return lax.ppermute(x, axes, pairs)  18.4 us
    all_to_all x1, blocking collectives, total_over(): return jnp.sum(lax.all_to_all(copies, axes, 0, 0, tiled=True), axis=0)  13.7 us
    all_to_all x1, starting transfers between devices, total_over(): return jnp.sum(lax.all_to_all(copies, axes, 0, 0, tiled=True), axis=0)  13.6 us
    all_to_all x1, waiting for transfers between devices, total_over(): return jnp.sum(lax.all_to_all(copies, axes, 0, 0, tiled=True), axis=0)  6.14 us
    pallas_call x1, Pallas kernels, relax(): pl.pallas_call(relax_kernel, out_shape=[field, field, jax.ShapeDtypeStruc...  4.55 us
    pallas_call x1, Pallas kernels, slabs(): pl.pallas_call(slab_kernel, out_shape=[jax.ShapeDtypeStruct((len(FIELDS),...  3.29 us
    pallas_call x1, Pallas kernels, faces(): pl.pallas_call(faces_kernel, out_shape=jax.ShapeDtypeStruct((3, PLANES, R...  3.27 us
  transfers between devices with their start and end apart: 5, of which 3 were waited for; matrix products, arithmetic and copies ran while one was open for 0% of the time, Pallas kernels for 3%

profile of v2, /device:TPU:1, one launch (start us, length us, event | category | flops | bytes accessed | tf_op | source)
XLA Modules:
  0.0 96.8 jit_solution(6367688003624566575)
XLA Ops:
  0.6 2.3 %strips.1 = (f32[8,24,256]{2,1,0:T(8,128)}, f32[8,24,256]{2,1,0:T(8,128)}) custom-call(f32[8,32,256]{2,1,0:T(8,128)} %al.5, f32[3,8,32,256]{3,2,1,0:T(8,128)} %ve.5, s32[3,8,32,256]{3,2,1,0:T(8,128)} %up.5, s32[8,32,256]{2,1,0:T(8,128)} %ct.5, f32[8,32,256]{2,1,0:T(8,128)} %la.5, f32[8,32,256]{2,1,0:T(8,128)} %lp.5, f32[8,32,256]{2,1,0:T(8,128)} %al.5, ...), custom_call_target="tpu_custom_call" | custom-call | tf_op jit(solution)/shard_map/strips/pallas_call | solution.py:124
  2.9 4.6 %collective-permute-start = (f32[8,24,256]{2,1,0:T(8,128)}, f32[8,24,256]{2,1,0:T(8,128)S(1)}, u32[]{:S(2)}, u32[]{:S(2)}) collective-permute-start(f32[8,24,256]{2,1,0:T(8,128)} %get-tuple-element.12), channel_id=1, source_target_pairs={{0,1},{1,2},{2,3},{3,4},{4,5},{5,6},{6,7},{8,9},{9,10},{10,11},{11... | collective-permute-start | bytes 589832 | tf_op jit(solution)/shard_map/ppermute | solution.py:38
  7.5 9.1 %collective-permute-start.1 = (f32[8,24,256]{2,1,0:T(8,128)}, f32[8,24,256]{2,1,0:T(8,128)S(1)}, u32[]{:S(2)}, u32[]{:S(2)}) collective-permute-start(f32[8,24,256]{2,1,0:T(8,128)} %get-tuple-element.13), channel_id=1, source_target_pairs={{1,0},{2,1},{3,2},{4,3},{5,4},{6,5},{7,6},{9,8},{10,9},{11,10},{12... | collective-permute-start | bytes 589832 | tf_op jit(solution)/shard_map/ppermute | solution.py:38
  16.6 0.0 collective-permute-done.prev
  16.6 0.0 copy-start.2
  16.7 1.2 %collective-permute-done.1.nxt = f32[8,24,256]{2,1,0:T(8,128)S(1)} collective-permute-done((f32[8,24,256]{2,1,0:T(8,128)}, f32[8,24,256]{2,1,0:T(8,128)S(1)}, u32[]{:S(2)}, u32[]{:S(2)}) %collective-permute-start.1) | collective-permute-done | bytes 196640 | tf_op jit(solution)/shard_map/ppermute | solution.py:38
  17.9 0.0 copy-done.2
  17.9 0.0 copy-start.3
  17.9 0.7 copy-done.3
  18.6 3.3 %slabs.1 = (f32[10,8,8,256]{3,2,1,0:T(8,128)}, f32[208,256]{1,0:T(8,128)}, f32[280,256]{1,0:T(8,128)}) custom-call(f32[8,32,256]{2,1,0:T(8,128)} %al.5, f32[3,8,32,256]{3,2,1,0:T(8,128)} %ve.5, s32[3,8,32,256]{3,2,1,0:T(8,128)} %up.5, s32[8,32,256]{2,1,0:T(8,128)} %ct.5, f32[8,32,256]{2,1,0:T(8,128)} %la.5, f32[8,32,256]{2,1,0:T(8,128)} %lp.5, ...), custom_call_target="tpu_custom_call" | custom-call | tf_op jit(solution)/shard_map/slabs/pallas_call | solution.py:255
  21.9 3.4 %collective-permute-start.2 = (f32[280,256]{1,0:T(8,128)}, f32[280,256]{1,0:T(8,128)S(1)}, u32[]{:S(2)}, u32[]{:S(2)}) collective-permute-start(f32[280,256]{1,0:T(8,128)} %get-tuple-element.15), channel_id=1, source_target_pairs={{0,8},{8,16},{16,24},{24,32},{32,40},{40,48},{48,56},{56,64},{64,7... | collective-permute-start | bytes 860168 | tf_op jit(solution)/shard_map/ppermute | solution.py:38
  25.2 1.3 %collective-permute-start.3 = (f32[208,256]{1,0:T(8,128)}, f32[208,256]{1,0:T(8,128)S(1)}, u32[]{:S(2)}, u32[]{:S(2)}) collective-permute-start(f32[208,256]{1,0:T(8,128)} %get-tuple-element.16), channel_id=1, source_target_pairs={{8,0},{16,8},{24,16},{32,24},{40,32},{48,40},{56,48},{64,56},{72,6... | collective-permute-start | bytes 638984 | tf_op jit(solution)/shard_map/ppermute | solution.py:38
  26.5 27.0 %collective-permute-done.3.above = f32[208,256]{1,0:T(8,128)S(1)} collective-permute-done((f32[208,256]{1,0:T(8,128)}, f32[208,256]{1,0:T(8,128)S(1)}, u32[]{:S(2)}, u32[]{:S(2)}) %collective-permute-start.3) | collective-permute-done | bytes 213024 | tf_op jit(solution)/shard_map/ppermute | solution.py:38
  53.6 0.0 copy-start
  53.6 0.0 collective-permute-done.2.below
  53.6 0.0 copy-start.1
  53.6 0.7 copy-done
  54.2 0.1 copy-done.1
  54.4 4.6 %relax.1 = (f32[8,32,256]{2,1,0:T(8,128)}, f32[8,32,256]{2,1,0:T(8,128)}, f32[32,128]{1,0:T(8,128)}) custom-call(f32[8,32,256]{2,1,0:T(8,128)} %al.5, f32[3,8,32,256]{3,2,1,0:T(8,128)} %ve.5, s32[3,8,32,256]{3,2,1,0:T(8,128)} %up.5, s32[8,32,256]{2,1,0:T(8,128)} %ct.5, f32[8,32,256]{2,1,0:T(8,128)} %la.5, f32[8,32,256]{2,1,0:T(8,128)} %lp.5, s32[32,256]{1,0:T(8,128)} %ow.1, ...), custom_call_target="tpu_custom_call" | custom-call | tf_op jit(solution)/shard_map/relax/pallas_call | solution.py:355
  58.9 13.7 %all_to_all.15 = f32[32,1,128]{2,1,0:T(1,128)S(1)} all-to-all(f32[32,1,128]{2,1,0:T(1,128)} %bitcast.5), channel_id=1, replica_groups=mesh['x'=4,'z'=12,'yh'=2,'yl'=4,'c'=2] {'x','yh','yl'}, dimensions={0} | all-to-all | bytes 32768 | tf_op jit(solution)/shard_map/all_to_all | solution.py:396
  72.6 0.1 reduce_sum.18
  72.7 0.6 broadcast_in_dim.2
  73.3 13.6 %all-to-all-start.1 = ((f32[24,1,128]{2,1,0:T(1,128)}), f32[24,1,128]{2,1,0:T(1,128)S(1)}, u32[]{:S(2)}, u32[]{:S(2)}) async-start(f32[24,1,128]{2,1,0:T(1,128)} %broadcast_in_dim.2), calls=%async_computation.1 | async-start | bytes 24576 | tf_op jit(solution)/shard_map/all_to_all | solution.py:396
  86.9 3.3 %faces.1 = f32[3,8,32,256]{3,2,1,0:T(8,128)} custom-call(f32[8,32,256]{2,1,0:T(8,128)} %al.5, f32[3,8,32,256]{3,2,1,0:T(8,128)} %ve.5, s32[3,8,32,256]{3,2,1,0:T(8,128)} %up.5, s32[8,32,256]{2,1,0:T(8,128)} %ct.5, f32[8,32,256]{2,1,0:T(8,128)} %la.5, f32[8,32,256]{2,1,0:T(8,128)} %lp.5, f32[10,8,8,256]{3,2,1,0:T(8,128)} %get-tuple-element.14.halo, ...), custom_call_target="tpu_custom_call" | custom-call | tf_op jit(solution)/shard_map/faces/pallas_call | solution.py:388
  90.1 6.1 %all-to-all-done.1 = f32[24,1,128]{2,1,0:T(1,128)S(1)} async-done(((f32[24,1,128]{2,1,0:T(1,128)}), f32[24,1,128]{2,1,0:T(1,128)S(1)}, u32[]{:S(2)}, u32[]{:S(2)}) %all-to-all-start.1) | async-done | bytes 12320 | tf_op jit(solution)/shard_map/all_to_all | solution.py:396
  96.3 0.5 slice_multiply_fusion
  (1 shorter events, 0.0 us)
Async XLA Ops:
  2.9 13.7 %collective-permute-start = (f32[8,24,256]{2,1,0:T(8,128)}, f32[8,24,256]{2,1,0:T(8,128)S(1)}, u32[]{:S(2)}, u32[]{:S(2)}) collective-permute-start(f32[8,24,256]{2,1,0:T(8,128)} %get-tuple-element.12), channel_id=1, source_target_pairs={{0,1},{1,2},{2,3},{3,4},{4,5},{5,6},{6,7},{8,9},{9,10},{10,11},{11... | collective-permute-start | bytes 589832 | tf_op jit(solution)/shard_map/ppermute | solution.py:38
  7.5 10.4 %collective-permute-start.1 = (f32[8,24,256]{2,1,0:T(8,128)}, f32[8,24,256]{2,1,0:T(8,128)S(1)}, u32[]{:S(2)}, u32[]{:S(2)}) collective-permute-start(f32[8,24,256]{2,1,0:T(8,128)} %get-tuple-element.13), channel_id=1, source_target_pairs={{1,0},{2,1},{3,2},{4,3},{5,4},{6,5},{7,6},{9,8},{10,9},{11,10},{12... | collective-permute-start | bytes 589832 | tf_op jit(solution)/shard_map/ppermute | solution.py:38
  16.6 1.3 %copy-start.2 = (f32[8,24,256]{2,1,0:T(8,128)}, f32[8,24,256]{2,1,0:T(8,128)S(1)}, u32[]{:S(2)}) copy-start(f32[8,24,256]{2,1,0:T(8,128)S(1)} %collective-permute-done.prev) | copy-start | bytes 589828
  17.9 0.7 copy-start.3
  21.9 31.7 %collective-permute-start.2 = (f32[280,256]{1,0:T(8,128)}, f32[280,256]{1,0:T(8,128)S(1)}, u32[]{:S(2)}, u32[]{:S(2)}) collective-permute-start(f32[280,256]{1,0:T(8,128)} %get-tuple-element.15), channel_id=1, source_target_pairs={{0,8},{8,16},{16,24},{24,32},{32,40},{40,48},{48,56},{56,64},{64,7... | collective-permute-start | bytes 860168 | tf_op jit(solution)/shard_map/ppermute | solution.py:38
  25.2 28.3 %collective-permute-start.3 = (f32[208,256]{1,0:T(8,128)}, f32[208,256]{1,0:T(8,128)S(1)}, u32[]{:S(2)}, u32[]{:S(2)}) collective-permute-start(f32[208,256]{1,0:T(8,128)} %get-tuple-element.16), channel_id=1, source_target_pairs={{8,0},{16,8},{24,16},{32,24},{40,32},{48,40},{56,48},{64,56},{72,6... | collective-permute-start | bytes 638984 | tf_op jit(solution)/shard_map/ppermute | solution.py:38
  53.6 0.7 copy-start
  53.6 0.8 copy-start.1
  73.3 23.0 %all-to-all-start.1 = ((f32[24,1,128]{2,1,0:T(1,128)}), f32[24,1,128]{2,1,0:T(1,128)S(1)}, u32[]{:S(2)}, u32[]{:S(2)}) async-start(f32[24,1,128]{2,1,0:T(1,128)} %broadcast_in_dim.2), calls=%async_computation.1 | async-start | bytes 24576 | tf_op jit(solution)/shard_map/all_to_all | solution.py:396

commit v3 on v2

v3 whole, which is shorter than its diff:
```python
import functools
import math

import jax
import jax.numpy as jnp
from jax import lax
from jax.experimental import pallas as pl
from jax.experimental.pallas import tpu as pltpu
from jax.sharding import Mesh
from jax.sharding import PartitionSpec as P

SWEEPS = 2
PORTS = 16
LEN = ("x", "z", "yh")
XS = ("yl", "c")
FIRST = ("x", "yh", "yl")
SECOND = ("z", "c")
SIZES = {"x": 4, "z": 12, "yh": 2, "yl": 4, "c": 2}
PLANES = 8
ROWS = 32
HALO = 8
EXT = ROWS + HALO
NZ = 256
WALL = 1e30
VMEM_LIMIT = 16 * 2**20
SLAB_FLOPS = 20_000_000
SLAB_BYTES = 40_000_000
STRIP = (("t", 3), ("al", 3), ("la", 3), ("lp", 2), ("c0", 2), ("m0", 2), ("c1", 3), ("m1", 2), ("c2", 2), ("m2", 2))
FIELDS = [name for name, _ in STRIP]
EARLY_ROWS = 7 * ROWS
DOWN_ROWS = 5 * ROWS + 2 * HALO
UP_ROWS = 4 * HALO
PARAMS = pltpu.CompilerParams(vmem_limit_bytes=VMEM_LIMIT)


def size_of(axes):
    return math.prod(SIZES[a] for a in axes)


def shift(x, axes, by):
    count = size_of(axes)
    pairs = [(i, i + by) for i in range(count) if 0 <= i + by < count]
    return lax.ppermute(x, axes, pairs)


def up_y(x):
    return pltpu.roll(x, EXT - 1, 0)


def down_y(x):
    return pltpu.roll(x, 1, 0)


def up_z(x):
    return pltpu.roll(x, NZ - 1, 1)


def down_z(x):
    return pltpu.roll(x, 1, 1)


def resistance(t, alpha):
    return jnp.where(t != 0.0, 1.0 + 9.0 * alpha, WALL)


def coupling(low, high):
    both = low + high
    through = both < 0.5 * WALL
    return through, jnp.where(through, 2.0 / both, 0.0)


def is_active(t):
    return jnp.abs(t) == 1.0


def split_flux(through, speed, donor, low, high):
    face = jnp.where(through, speed * (high - low), 0.0)
    stays = face * donor
    return stays, face - stays


def lanes(shape):
    return lax.broadcasted_iota(jnp.int32, shape, 1)


def sublanes(shape):
    return lax.broadcasted_iota(jnp.int32, shape, 0)


def strip_kernel(al, ve, up, ct, la, lp, to_next, to_prev, *scratch):
    sem = scratch[-1]
    last, first = scratch[:6], scratch[6:12]
    copies = []
    for kept, start in ((last, ROWS - HALO), (first, 0)):
        for source, target in zip((al, ve, up, ct, la, lp), kept):
            rows = pl.ds(start, HALO)
            window = source.at[:, rows, :] if len(source.shape) == 3 else source.at[:, :, rows, :]
            copies.append(pltpu.make_async_copy(window, target, sem.at[len(copies)]))
            copies[-1].start()
    for copy in copies:
        copy.wait()
    for out, kept, is_last in ((to_next, last, True), (to_prev, first, False)):
        al_k, ve_k, up_k, ct_k, la_k, lp_k = kept
        at = 0
        for name, count in STRIP:
            rows = pl.ds(HALO - count if is_last else 0, count)
            if name == "t":
                value = ct_k[:, rows, :].astype(jnp.float32) - 1.0
            elif name in ("al", "la", "lp"):
                value = {"al": al_k, "la": la_k, "lp": lp_k}[name][:, rows, :]
            elif name[0] == "c":
                value = 0.4 * ve_k[int(name[1]), :, rows, :]
                if name == "c1" and is_last:
                    donor = up_k[1, :, rows, :].astype(jnp.float32)
                    row = lax.broadcasted_iota(jnp.int32, value.shape, 1)
                    value = jnp.where(row == 0, value * (1.0 - donor), value)
            else:
                value = up_k[int(name[1]), :, rows, :].astype(jnp.float32)
            out[:, pl.ds(at, count), :] = value
            at += count


def strips(*args):
    message = jax.ShapeDtypeStruct((PLANES, 24, NZ), jnp.float32)
    kept = [pltpu.VMEM(x.shape[:-2] + (HALO, NZ), x.dtype) for x in args]
    return pl.pallas_call(
        strip_kernel,
        in_specs=[pl.BlockSpec(memory_space=pltpu.HBM)] * 6,
        out_shape=[message, message],
        scratch_shapes=kept + kept + [pltpu.SemaphoreType.DMA((12,))],
        compiler_params=PARAMS,
        name="strips",
    )(*(pltpu.with_memory_space_constraint(x, pltpu.HBM) for x in args))


class Own:
    def __init__(self, al, ve, up, ct, la, lp, halo):
        self.refs = (al, ve, up, ct, la, lp, halo)

    def get(self, name, p):
        al, ve, up, ct, la, lp, halo = self.refs
        if name == "t":
            own = ct[p].astype(jnp.float32) - 1.0
        elif name in ("al", "la", "lp"):
            own = {"al": al, "la": la, "lp": lp}[name][p]
        elif name[0] == "c":
            own = 0.4 * ve[int(name[1]), p]
        else:
            own = up[int(name[1]), p].astype(jnp.float32)
        tile = jnp.zeros((HALO, NZ), jnp.float32) if halo is None else halo[FIELDS.index(name), p]
        return jnp.concatenate([own, tile], axis=0)

    def resist(self, p):
        return resistance(self.get("t", p), self.get("al", p))


def in_plane(r):
    through_y, ky = coupling(r, up_y(r))
    through_z, kz = coupling(r, up_z(r))
    inside = lanes(r.shape) < NZ - 1
    return through_y, ky, through_z & inside, jnp.where(inside, kz, 0.0)


def in_plane_terms(own, p, r):
    through_y, ky, through_z, kz = in_plane(r)
    la = own.get("la", p)
    stays, passes = split_flux(through_y, own.get("c1", p), own.get("m1", p), la, up_y(la))
    flux = stays + down_y(passes)
    stays, passes = split_flux(through_z, own.get("c2", p), own.get("m2", p), la, up_z(la))
    flux = flux + (stays + down_z(passes))
    return flux, ky + down_y(ky), kz + down_z(kz), ky, kz


def between(own, p):
    through, k = coupling(own.resist(p), own.resist(p + 1))
    stays, passes = split_flux(through, own.get("c0", p), own.get("m0", p), own.get("la", p), own.get("la", p + 1))
    return k, stays, passes


def fill_halo(prev, nxt, halo):
    at = 0
    halo[...] = jnp.zeros(halo.shape, jnp.float32)
    for f, (_, count) in enumerate(STRIP):
        halo[f, :, pl.ds(0, count), :] = nxt[:, pl.ds(at, count), :]
        halo[f, :, pl.ds(HALO - count, count), :] = prev[:, pl.ds(at, count), :]
        at += count


def pack_pair(a, b):
    row = sublanes(a.shape)
    low = (row == 2) | (row == 3)
    high = (row == 4) | (row == 5)
    return jnp.where(low, pltpu.roll(b, 2, 0), jnp.where(high, pltpu.roll(b, HALO - 2, 0), a))


def pack_trio(a, b, c):
    row = sublanes(a.shape)
    out = jnp.where(row == 2, pltpu.roll(b, 2, 0), a)
    out = jnp.where(row == 5, pltpu.roll(b, HALO - 2, 0), out)
    out = jnp.where(row == 3, pltpu.roll(c, 3, 0), out)
    return jnp.where(row == 4, pltpu.roll(c, HALO - 3, 0), out)


def outer(a):
    row = sublanes(a.shape)
    return jnp.where((row < 2) | (row > 5), a, 0.0)


def unpack_pair(tile):
    row = sublanes(tile.shape)
    b = jnp.where(row < 2, pltpu.roll(tile, HALO - 2, 0), jnp.where(row > 5, pltpu.roll(tile, 2, 0), 0.0))
    return outer(tile), b


def unpack_trio(tile):
    row = sublanes(tile.shape)
    b = jnp.where(row == 0, pltpu.roll(tile, HALO - 2, 0), jnp.where(row == 7, pltpu.roll(tile, 2, 0), 0.0))
    c = jnp.where(row == 0, pltpu.roll(tile, HALO - 3, 0), jnp.where(row == 7, pltpu.roll(tile, 3, 0), 0.0))
    return outer(tile), b, c


def mobility(t, alpha):
    return jnp.where(t != 0.0, 1.0 / (1.0 + 9.0 * alpha), 0.0)


def resistance_of(mobile):
    return jnp.where(mobile > 0.0, 1.0 / mobile, WALL)


def weight(t, diag):
    return jnp.where(is_active(t) & (diag >= 0.5), 1.0 / diag, 0.0)


def with_coupling(scale, k):
    return scale / (1.0 + k * scale)


def edge_planes(own, edge, inner, far):
    low, lower_far = (edge, inner) if edge == 0 else (inner, far)
    k_edge, stays_edge, passes_edge = between(own, low)
    k_far, stays_far, passes_far = between(own, lower_far)
    if edge == 0:
        edge_flux, inner_flux = stays_edge, passes_edge + stays_far
    else:
        edge_flux, inner_flux = passes_edge, stays_edge + passes_far

    def sums(p, flux_len, k_len):
        flux, sum_y, sum_z, _, _ = in_plane_terms(own, p, own.resist(p))
        t = own.get("t", p)
        source = own.get("lp", p) + jnp.where(t != 0.0, own.get("la", p) + (flux_len + flux), 0.0)
        return source, weight(t, 0.5 + (k_len + sum_y + sum_z))

    source_in, weight_in = sums(inner, inner_flux, k_edge + k_far)
    carried = k_edge * (source_in * weight_in)
    source, scale = sums(edge, edge_flux, k_edge)
    return mobility(own.get("t", edge), own.get("al", edge)), own.get("la", edge), source, scale, carried


def early_kernel(al, ve, up, ct, la, lp, out):
    own = Own(al, ve, up, ct, la, lp, None)
    top = PLANES - 1
    planes = edge_planes(own, top, top - 1, top - 2) + (own.get("c0", top), own.get("m0", top))
    for i, plane in enumerate(planes):
        out[pl.ds(i * ROWS, ROWS), :] = plane[:ROWS]


def early(*args):
    return pl.pallas_call(
        early_kernel,
        out_shape=jax.ShapeDtypeStruct((EARLY_ROWS, NZ), jnp.float32),
        compiler_params=PARAMS,
        name="early",
    )(*args)


def end_rows(plane):
    return jnp.where(sublanes((HALO, NZ)) == 0, plane[:HALO], plane[ROWS - HALO : ROWS])


def slab_kernel(al, ve, up, ct, la, lp, prev, nxt, halo, down, upper):
    fill_halo(prev, nxt, halo)
    own = Own(al, ve, up, ct, la, lp, halo)
    top = PLANES - 1
    planes = edge_planes(own, 0, 1, 2)
    mobile, lam, source, scale, _ = planes
    for i, plane in enumerate(planes):
        down[pl.ds(i * ROWS, ROWS), :] = plane[:ROWS]
    down[pl.ds(5 * ROWS, HALO), :] = pack_trio(mobile[ROWS:], source[ROWS:], scale[ROWS:])
    down[pl.ds(5 * ROWS + HALO, HALO), :] = lam[ROWS:]
    mobile, lam, source, scale, carried = edge_planes(own, top, top - 1, top - 2)
    tiles = [
        pack_trio(mobile[ROWS:], source[ROWS:], scale[ROWS:]),
        pack_pair(lam[ROWS:], own.get("c0", top)[ROWS:]),
        own.get("m0", top)[ROWS:],
        pack_trio(end_rows(source), end_rows(scale), end_rows(carried)),
    ]
    for i, tile in enumerate(tiles):
        upper[pl.ds(i * HALO, HALO), :] = tile


def slabs(*args):
    return pl.pallas_call(
        slab_kernel,
        out_shape=[
            jax.ShapeDtypeStruct((len(FIELDS), PLANES, HALO, NZ), jnp.float32),
            jax.ShapeDtypeStruct((DOWN_ROWS, NZ), jnp.float32),
            jax.ShapeDtypeStruct((UP_ROWS, NZ), jnp.float32),
        ],
        compiler_params=PARAMS,
        cost_estimate=pl.CostEstimate(flops=SLAB_FLOPS, bytes_accessed=SLAB_BYTES, transcendentals=0),
        name="slabs",
    )(*args)


def joined(planes, halos):
    return [jnp.concatenate([a, b], axis=0) for a, b in zip(planes, halos)]


def rows_of(ref, count):
    return [ref[pl.ds(i * ROWS, ROWS), :] for i in range(count)]


def tiles_of(ref, planes, count):
    return [ref[pl.ds(planes * ROWS + i * HALO, HALO), :] for i in range(count)]


def read_above(ref):
    first, second = tiles_of(ref, 5, 2)
    mobile, source, scale = unpack_trio(first)
    return joined(rows_of(ref, 5), [mobile, outer(second), source, scale, jnp.zeros_like(first)])


def with_ends(plane, ends):
    row = sublanes((HALO, NZ))
    first = jnp.where(row == 0, ends, plane[:HALO])
    last = jnp.where(row == HALO - 1, ends, plane[ROWS - HALO :])
    return jnp.concatenate([first, plane[HALO : ROWS - HALO], last], axis=0)


def read_below(raw, ref):
    first, second, third, fourth = tiles_of(ref, 0, 4)
    mobile, source, scale = unpack_trio(first)
    lam, speed = unpack_pair(second)
    planes = rows_of(raw, 7)
    for i, ends in enumerate(unpack_trio(fourth)):
        planes[2 + i] = with_ends(planes[2 + i], ends)
    return joined(planes, [mobile, lam, source, scale, jnp.zeros_like(first), speed, outer(third)])


def sweep(i, x, source, scale, kl, ky, kz):
    mid = x(i)
    k_y, k_z = ky(i), kz(i)
    beside = k_y * up_y(mid) + down_y(k_y) * down_y(mid)
    beside = beside + (k_z * up_z(mid) + down_z(k_z) * down_z(mid))
    if i < PLANES:
        beside = beside + kl(i) * x(i + 1)
    if i >= 0:
        beside = beside + kl(i - 1) * x(i - 1)
    return (source(i) + beside) * scale(i)


def inner_kernel(al, ve, up, ct, la, lp, halo, grad, press, column, edges, source, scale, kl, ky, kz, first, second):
    own = Own(al, ve, up, ct, la, lp, halo)
    top = PLANES - 1
    incoming = 0.0
    for p in range(PLANES):
        r, t, lam = own.resist(p), own.get("t", p), own.get("la", p)
        flux, sum_y, sum_z, k_y, k_z = in_plane_terms(own, p, r)
        k_sum = sum_y + sum_z
        if p < top:
            k, stays, passes = between(own, p)
            kl[p] = k
            flux = flux + stays
            k_sum = k_sum + k
        if p > 0:
            flux = flux + incoming
            k_sum = k_sum + kl[p - 1]
        incoming = passes
        total = jnp.where(t != 0.0, lam + flux, 0.0)
        grad[p] = total[:ROWS]
        ky[p], kz[p] = k_y, k_z
        source[p] = own.get("lp", p) + total
        scale[p] = weight(t, 0.5 + k_sum)
        first[p] = source[p] * scale[p]
    kl[top] = jnp.zeros((EXT, NZ), jnp.float32)
    kept = (own.resist(0), own.get("la", 0), own.resist(top), own.get("la", top), own.get("c0", top), own.get("m0", top))
    for i, plane in enumerate(kept):
        edges[i] = plane

    def at(ref):
        return lambda i: ref[i]

    coefficients = [at(ref) for ref in (source, scale, kl, ky, kz)]
    zero = jnp.zeros((EXT, NZ), jnp.float32)
    for p in range(PLANES):
        second[p] = sweep(p, at(first), *coefficients) if 2 <= p < PLANES - 2 else zero
    total = jnp.zeros((ROWS, NZ), jnp.float32)
    for p in range(PLANES):
        if 3 <= p < PLANES - 3:
            x = sweep(p, at(second), *coefficients)[:ROWS]
            total = total + jnp.where(ct[p] == 2, la[p] + x, 0.0)
        else:
            x = zero[:ROWS]
        press[p] = x
    column[...] = total


def inner(args, halo):
    field = jax.ShapeDtypeStruct((PLANES, ROWS, NZ), jnp.float32)
    wide = jax.ShapeDtypeStruct((PLANES, EXT, NZ), jnp.float32)
    kept = jax.ShapeDtypeStruct((6, EXT, NZ), jnp.float32)
    return pl.pallas_call(
        inner_kernel,
        out_shape=[field, field, jax.ShapeDtypeStruct((ROWS, NZ), jnp.float32), kept] + [wide] * 7,
        compiler_params=PARAMS,
        cost_estimate=pl.CostEstimate(flops=20_000_000, bytes_accessed=6_000_000, transcendentals=0),
        name="inner",
    )(*args, halo)


def relax_kernel(
    ct, la, ow, raw, below, above, grad_in, press_in, column_in, edges, source, scale, kl, ky, kz, first, second,
    grad, press, sums,
):
    top = PLANES - 1
    s_b, la_b, src_b, w_b, carried_b, c_b, m_b = read_below(raw, below)
    s_a, la_a, src_a, w_a, carried_a = read_above(above)
    r_b, r_a = resistance_of(s_b), resistance_of(s_a)
    r_0, la_0, r_7, la_7, c_7, m_7 = (edges[i] for i in range(6))
    through, k_b = coupling(r_b, r_0)
    stays_b, passes_b = split_flux(through, c_b, m_b, la_b, la_0)
    through, k_a = coupling(r_7, r_a)
    stays_a, passes_a = split_flux(through, c_7, m_7, la_7, la_a)
    _, ky_b, _, kz_b = in_plane(r_b)
    _, ky_a, _, kz_a = in_plane(r_a)

    def at(ref, changed):
        return lambda i: changed[i] if i in changed else ref[i]

    sources = {-1: src_b + stays_b, 0: source[0] + passes_b, top: source[top] + stays_a, PLANES: src_a + passes_a}
    scales = {-1: with_coupling(w_b, k_b), 0: with_coupling(scale[0], k_b)}
    scales |= {top: with_coupling(scale[top], k_a), PLANES: with_coupling(w_a, k_a)}
    x = at(first, {i: sources[i] * scales[i] for i in sources})
    sources[-1] = sources[-1] + carried_b
    sources[PLANES] = sources[PLANES] + carried_a
    coefficients = (
        at(source, sources),
        at(scale, scales),
        at(kl, {-1: k_b, top: k_a}),
        at(ky, {-1: ky_b, PLANES: ky_a}),
        at(kz, {-1: kz_b, PLANES: kz_a}),
    )
    done = range(2, PLANES - 2)
    x = at(second, {i: sweep(i, x, *coefficients) for i in range(-1, PLANES + 1) if i not in done})
    done = range(3, PLANES - 3)
    column = column_in[...]
    for p in range(PLANES):
        if p in done:
            press[p] = press_in[p]
        else:
            value = sweep(p, x, *coefficients)[:ROWS]
            press[p] = value
            column = column + jnp.where(ct[p] == 2, la[p] + value, 0.0)
        grad[p] = grad_in[p]
    grad[0] = grad_in[0] + passes_b[:ROWS]
    grad[top] = grad_in[top] + stays_a[:ROWS]
    owner = ow[...]
    parts = []
    for port in range(PORTS):
        mine = jnp.where(owner == port, column, 0.0)
        mine = mine[:, :128] + mine[:, 128:]
        parts.append(jnp.sum(mine, axis=0, keepdims=True))
    table = jnp.sum(jnp.concatenate(parts, axis=0), axis=1, keepdims=True)
    diagonal = lanes((PORTS, 128)) == sublanes((PORTS, 128))
    line = jnp.sum(jnp.where(diagonal, table, 0.0), axis=0, keepdims=True)
    sums[...] = jnp.broadcast_to(line, sums.shape)


def relax(celltype, lam, owner, raw, below, above, inside):
    field = jax.ShapeDtypeStruct((PLANES, ROWS, NZ), jnp.float32)
    return pl.pallas_call(
        relax_kernel,
        out_shape=[field, field, jax.ShapeDtypeStruct((size_of(FIRST), 128), jnp.float32)],
        compiler_params=PARAMS,
        name="relax",
    )(celltype, lam, owner, raw, below, above, *inside)


def faces_kernel(al, ve, up, ct, la, lp, halo, above, out):
    own = Own(al, ve, up, ct, la, lp, halo)
    mobile, la_a = read_above(above)[:2]
    r_a = resistance_of(mobile)
    al_a = (r_a - 1.0) / 9.0

    def write(axis, p, through, speed, donor, lam, lam_next, alpha, alpha_next):
        face = jnp.where(through, speed * (lam_next - lam), 0.0)
        out[axis, p] = (face * jnp.where(donor != 0.0, alpha, alpha_next))[:ROWS]

    for p in range(PLANES):
        r, alpha, lam = own.resist(p), own.get("al", p), own.get("la", p)
        inner = p < PLANES - 1
        r_next = own.resist(p + 1) if inner else r_a
        alpha_next = own.get("al", p + 1) if inner else al_a
        lam_next = own.get("la", p + 1) if inner else la_a
        through, _ = coupling(r, r_next)
        write(0, p, through, own.get("c0", p), own.get("m0", p), lam, lam_next, alpha, alpha_next)
        through, _ = coupling(r, up_y(r))
        write(1, p, through, own.get("c1", p), own.get("m1", p), lam, up_y(lam), alpha, up_y(alpha))
        through, _ = coupling(r, up_z(r))
        through = through & (lanes(r.shape) < NZ - 1)
        write(2, p, through, own.get("c2", p), own.get("m2", p), lam, up_z(lam), alpha, up_z(alpha))


def faces(alpha, velocity, upwind, celltype, lam, lam_press, halo, above):
    return pl.pallas_call(
        faces_kernel,
        out_shape=jax.ShapeDtypeStruct((3, PLANES, ROWS, NZ), jnp.float32),
        compiler_params=PARAMS,
        cost_estimate=pl.CostEstimate(flops=5_000_000, bytes_accessed=4_000_000, transcendentals=0),
        name="faces",
    )(alpha, velocity, upwind, celltype, lam, lam_press, halo, above)


def total_over(copies, axes):
    return jnp.sum(lax.all_to_all(copies, axes, 0, 0, tiled=True), axis=0)


def body(alpha, velocity, upwind, celltype, owner, lam_alpha, lam_press):
    args = (alpha, velocity, upwind, celltype, lam_alpha, lam_press)
    to_next, to_prev = strips(*args)
    prev = shift(to_next, XS, 1)
    nxt = shift(to_prev, XS, -1)
    raw = shift(early(*args), LEN, 1)
    halo, down, upper = slabs(*args, prev, nxt)
    above = shift(down, LEN, -1)
    below = shift(upper, LEN, 1)
    inside = inner(args, halo)
    grad_alpha, press, sums = relax(celltype, lam_alpha, owner, raw, below, above, inside)
    grad_velocity = faces(*args, halo, above)
    sums = total_over(sums, FIRST)
    sums = total_over(jnp.broadcast_to(sums[None], (size_of(SECOND), 128)), SECOND)
    cells = math.prod(alpha.shape) * size_of(LEN + XS)
    return (grad_alpha, grad_velocity, press, sums[:PORTS] / math.sqrt(cells))


def solution(mesh):
    parts = Mesh(mesh.devices.reshape(tuple(SIZES.values())), tuple(SIZES))
    field = P(LEN, XS, None)
    faces_spec = P(None, LEN, XS, None)
    in_specs = (field, faces_spec, faces_spec, field, P(XS, None), field, field)
    out_specs = (field, faces_spec, field, P())
    return jax.shard_map(body, mesh=parts, in_specs=in_specs, out_specs=out_specs, check_vma=False)
```

time: 97.2 us -> 85.5 us (0.88)
  waiting for transfers between devices: 34.4 us -> 21.9 us
  starting transfers between devices: 31.9 us -> 39.2 us
  Pallas kernels: 13.4 us -> 6.52 us
  blocking collectives: 13.7 us -> 15.6 us
  local copies, waits for them, and re-layouts: 2.06 us -> 0.64 us
    ppermute x4 -> x5, waiting for transfers between devices: 28.3 us -> 13.8 us  [shift(): return lax.ppermute(x, axes, pairs)]
    ppermute x4 -> x5, starting transfers between devices: 18.4 us -> 24.2 us  [shift(): return lax.ppermute(x, axes, pairs)]
    pallas_call x1, Pallas kernels: 4.55 us -> 1.38 us  [relax(): pl.pallas_call(relax_kernel, out_shape=[field, field, jax.ShapeDtypeStruc...]
    pallas_call x1, Pallas kernels: 3.29 us -> 0.53 us  [slabs(): pl.pallas_call(slab_kernel, out_shape=[jax.ShapeDtypeStruct((len(FIELDS),...]
    all_to_all x1, waiting for transfers between devices: 6.14 us -> 8.06 us  [total_over(): return jnp.sum(lax.all_to_all(copies, axes, 0, 0, tiled=True), axis=0)]
    pallas_call x1, Pallas kernels: 3.27 us -> 1.35 us  [faces(): pl.pallas_call(faces_kernel, out_shape=jax.ShapeDtypeStruct((3, PLANES, R...]
    all_to_all x1, blocking collectives: 13.7 us -> 15.6 us  [total_over(): return jnp.sum(lax.all_to_all(copies, axes, 0, 0, tiled=True), axis=0)]
    unnamed x8 -> x14, local copies, waits for them, and re-layouts: 1.46 us -> 0.03 us
  transfers between devices with their start and end apart: 5 -> 6, of which waited for: 3 -> 3; matrix products, arithmetic and copies ran while one was open for 0% -> 0% of each run, Pallas kernels for 3% -> 4%
where the time goes in v3:
time: 85.5 us; the launch traced here: 85.2 us
  starting transfers between devices  39.2 us (46%)
  waiting for transfers between devices  21.9 us (26%)
  blocking collectives  15.6 us (18%)
  Pallas kernels  6.52 us (8%)
    ppermute x5, starting transfers between devices, shift(): return lax.ppermute(x, axes, pairs)  24.2 us
    all_to_all x1, blocking collectives, total_over(): return jnp.sum(lax.all_to_all(copies, axes, 0, 0, tiled=True), axis=0)  15.6 us
    all_to_all x1, starting transfers between devices, total_over(): return jnp.sum(lax.all_to_all(copies, axes, 0, 0, tiled=True), axis=0)  15 us
    ppermute x5, waiting for transfers between devices, shift(): return lax.ppermute(x, axes, pairs)  13.8 us
    all_to_all x1, waiting for transfers between devices, total_over(): return jnp.sum(lax.all_to_all(copies, axes, 0, 0, tiled=True), axis=0)  8.06 us
    pallas_call x1, Pallas kernels, strips(): pl.pallas_call(strip_kernel, in_specs=[pl.BlockSpec(memory_space=pltpu.HB...  1.75 us
  transfers between devices with their start and end apart: 6, of which 3 were waited for; matrix products, arithmetic and copies ran while one was open for 0% of the time, Pallas kernels for 4%

profile of v3, /device:TPU:1, one launch (start us, length us, event | category | flops | bytes accessed | tf_op | source)
XLA Modules:
  0.0 85.2 jit_solution(2263684430364418855)
XLA Ops:
  0.6 0.0 copy-start.2
  0.6 0.0 copy-start.3
  0.7 0.0 copy-start.5
  0.7 0.0 copy-start.4
  0.7 0.0 copy-start
  0.7 0.0 copy-start.1
  0.7 1.7 %strips.1 = (f32[8,24,256]{2,1,0:T(8,128)S(1)}, f32[8,24,256]{2,1,0:T(8,128)S(1)}) custom-call(f32[8,32,256]{2,1,0:T(8,128)} %al.9, f32[3,8,32,256]{3,2,1,0:T(8,128)} %ve.9, s32[3,8,32,256]{3,2,1,0:T(8,128)} %up.9, s32[8,32,256]{2,1,0:T(8,128)} %ct.11, f32[8,32,256]{2,1,0:T(8,128)} %la.11, f32[8,32,256]{2,1,0:T(8,128)} %lp.9), custom_call_target="tpu_custom_call" | custom-call | tf_op jit(solution)/shard_map/strips/pallas_call | solution.py:126
  2.4 4.6 %collective-permute-start.1 = (f32[8,24,256]{2,1,0:T(8,128)S(1)}, f32[8,24,256]{2,1,0:T(8,128)S(1)}, u32[]{:S(2)}, u32[]{:S(2)}) collective-permute-start(f32[8,24,256]{2,1,0:T(8,128)S(1)} %get-tuple-element.23), channel_id=1, source_target_pairs={{0,1},{1,2},{2,3},{3,4},{4,5},{5,6},{6,7},{8,9},{9,10},{10,11},{11... | collective-permute-start | bytes 589832 | tf_op jit(solution)/shard_map/ppermute | solution.py:43
  7.0 9.1 %collective-permute-start.2 = (f32[8,24,256]{2,1,0:T(8,128)S(1)}, f32[8,24,256]{2,1,0:T(8,128)S(1)}, u32[]{:S(2)}, u32[]{:S(2)}) collective-permute-start(f32[8,24,256]{2,1,0:T(8,128)S(1)} %get-tuple-element.24), channel_id=1, source_target_pairs={{1,0},{2,1},{3,2},{4,3},{5,4},{6,5},{7,6},{9,8},{10,9},{11,10},{12... | collective-permute-start | bytes 589832 | tf_op jit(solution)/shard_map/ppermute | solution.py:43
  16.2 0.0 copy-done.2
  16.2 0.0 copy-done.3
  16.2 0.0 copy-done.5
  16.2 0.0 copy-done.4
  16.2 0.0 copy-done
  16.2 0.0 copy-done.1
  16.2 0.2 early.1
  16.5 1.3 %collective-permute-start = (f32[224,256]{1,0:T(8,128)S(1)}, f32[224,256]{1,0:T(8,128)S(1)}, u32[]{:S(2)}, u32[]{:S(2)}) collective-permute-start(f32[224,256]{1,0:T(8,128)S(1)} %early.1), channel_id=1, source_target_pairs={{0,8},{8,16},{16,24},{24,32},{32,40},{40,48},{48,56},{56,64},{64,7... | collective-permute-start | bytes 688136 | tf_op jit(solution)/shard_map/ppermute | solution.py:43
  17.8 0.0 collective-permute-done.1.prev
  17.8 0.0 collective-permute-done.2.nxt
  17.8 0.5 slabs.1
  18.4 1.3 %collective-permute-start.4 = (f32[176,256]{1,0:T(8,128)S(1)}, f32[176,256]{1,0:T(8,128)S(1)}, u32[]{:S(2)}, u32[]{:S(2)}) collective-permute-start(f32[176,256]{1,0:T(8,128)S(1)} %get-tuple-element.26), channel_id=1, source_target_pairs={{8,0},{16,8},{24,16},{32,24},{40,32},{48,40},{56,48},{64,56},{72,6... | collective-permute-start | bytes 540680 | tf_op jit(solution)/shard_map/ppermute | solution.py:43
  19.7 7.9 %collective-permute-start.3 = (f32[32,256]{1,0:T(8,128)S(1)}, f32[32,256]{1,0:T(8,128)S(1)}, u32[]{:S(2)}, u32[]{:S(2)}) collective-permute-start(f32[32,256]{1,0:T(8,128)S(1)} %get-tuple-element.25), channel_id=1, source_target_pairs={{0,8},{8,16},{16,24},{24,32},{32,40},{40,48},{48,56},{56,64},{64,7... | collective-permute-start | bytes 98312 | tf_op jit(solution)/shard_map/ppermute | solution.py:43
  27.6 0.0 copy-start.6
  27.6 1.3 %inner.1 = (f32[8,32,256]{2,1,0:T(8,128)S(1)}, f32[8,32,256]{2,1,0:T(8,128)S(1)}, f32[32,256]{1,0:T(8,128)S(1)}, f32[6,40,256]{2,1,0:T(8,128)S(1)}, f32[8,40,256...) custom-call(f32[8,32,256]{2,1,0:T(8,128)S(1)} %copy-done.4, ...), custom_call_target="tpu_custom_call" | custom-call | flops 20000000 | bytes 6000000 | tf_op jit(solution)/shard_map/inner/pallas_call | solution.py:412
  28.9 4.9 %collective-permute-done.3.below = f32[32,256]{1,0:T(8,128)S(1)} collective-permute-done((f32[32,256]{1,0:T(8,128)S(1)}, f32[32,256]{1,0:T(8,128)S(1)}, u32[]{:S(2)}, u32[]{:S(2)}) %collective-permute-start.3) | collective-permute-done | bytes 32800 | tf_op jit(solution)/shard_map/ppermute | solution.py:43
  33.8 0.0 collective-permute-done.raw
  33.8 8.8 %collective-permute-done.4.above = f32[176,256]{1,0:T(8,128)S(1)} collective-permute-done((f32[176,256]{1,0:T(8,128)S(1)}, f32[176,256]{1,0:T(8,128)S(1)}, u32[]{:S(2)}, u32[]{:S(2)}) %collective-permute-start.4) | collective-permute-done | bytes 180256 | tf_op jit(solution)/shard_map/ppermute | solution.py:43
  42.6 0.0 copy-done.6
  42.6 1.4 %relax.1 = (f32[8,32,256]{2,1,0:T(8,128)}, f32[8,32,256]{2,1,0:T(8,128)}, f32[32,128]{1,0:T(8,128)S(1)}) custom-call(s32[8,32,256]{2,1,0:T(8,128)S(1)} %copy-done.2, f32[8,32,256]{2,1,0:T(8,128)S(1)} %copy-done.3, s32[32,256]{1,0:T(8,128)S(1)} %copy-done.6, f32[224,256]{1,0:T(8,128)S(1)} %collective-permute-done.raw, ...), custom_call_target="tpu_custom_call" | custom-call | tf_op jit(solution)/shard_map/relax/pallas_call | solution.py:481
  44.0 15.6 %all_to_all.15 = f32[32,1,128]{2,1,0:T(1,128)S(1)} all-to-all(f32[32,1,128]{2,1,0:T(1,128)S(1)} %bitcast.4), channel_id=1, replica_groups=mesh['x'=4,'z'=12,'yh'=2,'yl'=4,'c'=2] {'x','yh','yl'}, dimensions={0} | all-to-all | bytes 32768 | tf_op jit(solution)/shard_map/all_to_all | solution.py:525
  59.6 0.1 reduce_sum.18
  59.7 0.6 broadcast_in_dim.2
  60.3 15.0 %all-to-all-start.1 = ((f32[24,1,128]{2,1,0:T(1,128)}), f32[24,1,128]{2,1,0:T(1,128)S(1)}, u32[]{:S(2)}, u32[]{:S(2)}) async-start(f32[24,1,128]{2,1,0:T(1,128)} %broadcast_in_dim.2), calls=%async_computation.1 | async-start | bytes 24576 | tf_op jit(solution)/shard_map/all_to_all | solution.py:525
  75.3 1.4 %faces.1 = f32[3,8,32,256]{3,2,1,0:T(8,128)} custom-call(f32[8,32,256]{2,1,0:T(8,128)S(1)} %copy-done.4, f32[3,8,32,256]{3,2,1,0:T(8,128)S(1)} %copy-done, s32[3,8,32,256]{3,2,1,0:T(8,128)S(1)} %copy-done.1, s32[8,32,256]{2,1,0:T(8,128)S(1)} %copy-done.2, f32[8,32,256]{2,1,0:T(8,128)S(1)} %copy-done.3, f32[8,32,256]{2,1,0:T(8,128)S(1)} %copy-done.5, ...), custom_call_target="tpu_custom_call" | custom-call | flops 5000000 | bytes 4000000 | tf_op jit(solution)/shard_map/faces/pallas_call | solution.py:515
  76.6 8.1 %all-to-all-done.1 = f32[24,1,128]{2,1,0:T(1,128)S(1)} async-done(((f32[24,1,128]{2,1,0:T(1,128)}), f32[24,1,128]{2,1,0:T(1,128)S(1)}, u32[]{:S(2)}, u32[]{:S(2)}) %all-to-all-start.1) | async-done | bytes 12320 | tf_op jit(solution)/shard_map/all_to_all | solution.py:525
  84.7 0.5 slice_multiply_fusion
  (1 shorter events, 0.0 us)
Async XLA Ops:
  0.6 15.6 %copy-start.2 = (s32[8,32,256]{2,1,0:T(8,128)S(1)}, s32[8,32,256]{2,1,0:T(8,128)}, u32[]{:S(2)}) copy-start(s32[8,32,256]{2,1,0:T(8,128)} %ct.11) | copy-start | bytes 786436
  0.6 15.6 %copy-start.3 = (f32[8,32,256]{2,1,0:T(8,128)S(1)}, f32[8,32,256]{2,1,0:T(8,128)}, u32[]{:S(2)}) copy-start(f32[8,32,256]{2,1,0:T(8,128)} %la.11) | copy-start | bytes 786436
  0.7 15.6 %copy-start.5 = (f32[8,32,256]{2,1,0:T(8,128)S(1)}, f32[8,32,256]{2,1,0:T(8,128)}, u32[]{:S(2)}) copy-start(f32[8,32,256]{2,1,0:T(8,128)} %lp.9) | copy-start | bytes 786436
  0.7 15.6 %copy-start.4 = (f32[8,32,256]{2,1,0:T(8,128)S(1)}, f32[8,32,256]{2,1,0:T(8,128)}, u32[]{:S(2)}) copy-start(f32[8,32,256]{2,1,0:T(8,128)} %al.9) | copy-start | bytes 786436
  0.7 15.6 %copy-start = (f32[3,8,32,256]{3,2,1,0:T(8,128)S(1)}, f32[3,8,32,256]{3,2,1,0:T(8,128)}, u32[]{:S(2)}) copy-start(f32[3,8,32,256]{3,2,1,0:T(8,128)} %ve.9) | copy-start | bytes 2359300
  0.7 15.6 %copy-start.1 = (s32[3,8,32,256]{3,2,1,0:T(8,128)S(1)}, s32[3,8,32,256]{3,2,1,0:T(8,128)}, u32[]{:S(2)}) copy-start(s32[3,8,32,256]{3,2,1,0:T(8,128)} %up.9) | copy-start | bytes 2359300
  2.4 15.4 %collective-permute-start.1 = (f32[8,24,256]{2,1,0:T(8,128)S(1)}, f32[8,24,256]{2,1,0:T(8,128)S(1)}, u32[]{:S(2)}, u32[]{:S(2)}) collective-permute-start(f32[8,24,256]{2,1,0:T(8,128)S(1)} %get-tuple-element.23), channel_id=1, source_target_pairs={{0,1},{1,2},{2,3},{3,4},{4,5},{5,6},{6,7},{8,9},{9,10},{10,11},{11... | collective-permute-start | bytes 589832 | tf_op jit(solution)/shard_map/ppermute | solution.py:43
  7.0 10.8 %collective-permute-start.2 = (f32[8,24,256]{2,1,0:T(8,128)S(1)}, f32[8,24,256]{2,1,0:T(8,128)S(1)}, u32[]{:S(2)}, u32[]{:S(2)}) collective-permute-start(f32[8,24,256]{2,1,0:T(8,128)S(1)} %get-tuple-element.24), channel_id=1, source_target_pairs={{1,0},{2,1},{3,2},{4,3},{5,4},{6,5},{7,6},{9,8},{10,9},{11,10},{12... | collective-permute-start | bytes 589832 | tf_op jit(solution)/shard_map/ppermute | solution.py:43
  16.5 17.3 %collective-permute-start = (f32[224,256]{1,0:T(8,128)S(1)}, f32[224,256]{1,0:T(8,128)S(1)}, u32[]{:S(2)}, u32[]{:S(2)}) collective-permute-start(f32[224,256]{1,0:T(8,128)S(1)} %early.1), channel_id=1, source_target_pairs={{0,8},{8,16},{16,24},{24,32},{32,40},{40,48},{48,56},{56,64},{64,7... | collective-permute-start | bytes 688136 | tf_op jit(solution)/shard_map/ppermute | solution.py:43
  18.4 24.3 %collective-permute-start.4 = (f32[176,256]{1,0:T(8,128)S(1)}, f32[176,256]{1,0:T(8,128)S(1)}, u32[]{:S(2)}, u32[]{:S(2)}) collective-permute-start(f32[176,256]{1,0:T(8,128)S(1)} %get-tuple-element.26), channel_id=1, source_target_pairs={{8,0},{16,8},{24,16},{32,24},{40,32},{48,40},{56,48},{64,56},{72,6... | collective-permute-start | bytes 540680 | tf_op jit(solution)/shard_map/ppermute | solution.py:43
  19.7 14.1 %collective-permute-start.3 = (f32[32,256]{1,0:T(8,128)S(1)}, f32[32,256]{1,0:T(8,128)S(1)}, u32[]{:S(2)}, u32[]{:S(2)}) collective-permute-start(f32[32,256]{1,0:T(8,128)S(1)} %get-tuple-element.25), channel_id=1, source_target_pairs={{0,8},{8,16},{16,24},{24,32},{32,40},{40,48},{48,56},{56,64},{64,7... | collective-permute-start | bytes 98312 | tf_op jit(solution)/shard_map/ppermute | solution.py:43
  27.6 15.1 %copy-start.6 = (s32[32,256]{1,0:T(8,128)S(1)}, s32[32,256]{1,0:T(8,128)}, u32[]{:S(2)}) copy-start(s32[32,256]{1,0:T(8,128)} %ow.1) | copy-start | bytes 98308
  60.3 24.4 %all-to-all-start.1 = ((f32[24,1,128]{2,1,0:T(1,128)}), f32[24,1,128]{2,1,0:T(1,128)S(1)}, u32[]{:S(2)}, u32[]{:S(2)}) async-start(f32[24,1,128]{2,1,0:T(1,128)} %broadcast_in_dim.2), calls=%async_computation.1 | async-start | bytes 24576 | tf_op jit(solution)/shard_map/all_to_all | solution.py:525

commit v4 on v3

--- a/solution.py
+++ b/solution.py
@@ -43,6 +43,15 @@
     return lax.ppermute(x, axes, pairs)
 
 
+def swap(x, axes, first):
+    pairs = [(i, i + 1) for i in range(first, size_of(axes) - 1, 2)]
+    return lax.ppermute(x, axes, pairs + [(j, i) for i, j in pairs])
+
+
+def is_lower():
+    return lax.axis_index("c") == 0
+
+
 def up_y(x):
     return pltpu.roll(x, EXT - 1, 0)
 
@@ -87,7 +96,7 @@
     return lax.broadcasted_iota(jnp.int32, shape, 0)
 
 
-def strip_kernel(al, ve, up, ct, la, lp, to_next, to_prev, *scratch):
+def strip_kernel(al, ve, up, ct, la, lp, in_chip, off_chip, *scratch):
     sem = scratch[-1]
     last, first = scratch[:6], scratch[6:12]
     copies = []
@@ -99,25 +108,29 @@
             copies[-1].start()
     for copy in copies:
         copy.wait()
-    for out, kept, is_last in ((to_next, last, True), (to_prev, first, False)):
+    def value_of(name, count, kept, is_last):
         al_k, ve_k, up_k, ct_k, la_k, lp_k = kept
-        at = 0
-        for name, count in STRIP:
-            rows = pl.ds(HALO - count if is_last else 0, count)
-            if name == "t":
-                value = ct_k[:, rows, :].astype(jnp.float32) - 1.0
-            elif name in ("al", "la", "lp"):
-                value = {"al": al_k, "la": la_k, "lp": lp_k}[name][:, rows, :]
-            elif name[0] == "c":
-                value = 0.4 * ve_k[int(name[1]), :, rows, :]
-                if name == "c1" and is_last:
-                    donor = up_k[1, :, rows, :].astype(jnp.float32)
-                    row = lax.broadcasted_iota(jnp.int32, value.shape, 1)
-                    value = jnp.where(row == 0, value * (1.0 - donor), value)
-            else:
-                value = up_k[int(name[1]), :, rows, :].astype(jnp.float32)
-            out[:, pl.ds(at, count), :] = value
-            at += count
+        rows = pl.ds(HALO - count if is_last else 0, count)
+        if name == "t":
+            return ct_k[:, rows, :].astype(jnp.float32) - 1.0
+        if name in ("al", "la", "lp"):
+            return {"al": al_k, "la": la_k, "lp": lp_k}[name][:, rows, :]
+        if name[0] == "m":
+            return up_k[int(name[1]), :, rows, :].astype(jnp.float32)
+        value = 0.4 * ve_k[int(name[1]), :, rows, :]
+        if name == "c1" and is_last:
+            donor = up_k[1, :, rows, :].astype(jnp.float32)
+            row = lax.broadcasted_iota(jnp.int32, value.shape, 1)
+            value = jnp.where(row == 0, value * (1.0 - donor), value)
+        return value
+
+    at = 0
+    for name, count in STRIP:
+        to_next = value_of(name, count, last, True)
+        to_prev = value_of(name, count, first, False)
+        in_chip[:, pl.ds(at, count), :] = jnp.where(is_lower(), to_next, to_prev)
+        off_chip[:, pl.ds(at, count), :] = jnp.where(is_lower(), to_prev, to_next)
+        at += count
 
 
 def strips(*args):
@@ -177,12 +190,14 @@
     return k, stays, passes
 
 
-def fill_halo(prev, nxt, halo):
+def fill_halo(in_chip, off_chip, halo):
+    prev = jnp.where(is_lower(), off_chip[...], in_chip[...])
+    nxt = jnp.where(is_lower(), in_chip[...], off_chip[...])
     at = 0
     halo[...] = jnp.zeros(halo.shape, jnp.float32)
     for f, (_, count) in enumerate(STRIP):
-        halo[f, :, pl.ds(0, count), :] = nxt[:, pl.ds(at, count), :]
-        halo[f, :, pl.ds(HALO - count, count), :] = prev[:, pl.ds(at, count), :]
+        halo[f, :, pl.ds(0, count), :] = nxt[:, at : at + count, :]
+        halo[f, :, pl.ds(HALO - count, count), :] = prev[:, at : at + count, :]
         at += count
 
 
@@ -277,8 +292,8 @@
     return jnp.where(sublanes((HALO, NZ)) == 0, plane[:HALO], plane[ROWS - HALO : ROWS])
 
 
-def slab_kernel(al, ve, up, ct, la, lp, prev, nxt, halo, down, upper):
-    fill_halo(prev, nxt, halo)
+def slab_kernel(al, ve, up, ct, la, lp, in_chip, off_chip, halo, down, upper):
+    fill_halo(in_chip, off_chip, halo)
     own = Own(al, ve, up, ct, la, lp, halo)
     top = PLANES - 1
     planes = edge_planes(own, 0, 1, 2)
@@ -527,11 +542,11 @@
 
 def body(alpha, velocity, upwind, celltype, owner, lam_alpha, lam_press):
     args = (alpha, velocity, upwind, celltype, lam_alpha, lam_press)
-    to_next, to_prev = strips(*args)
-    prev = shift(to_next, XS, 1)
-    nxt = shift(to_prev, XS, -1)
+    in_chip, off_chip = strips(*args)
+    in_chip = swap(in_chip, XS, 0)
+    off_chip = swap(off_chip, XS, 1)
     raw = shift(early(*args), LEN, 1)
-    halo, down, upper = slabs(*args, prev, nxt)
+    halo, down, upper = slabs(*args, in_chip, off_chip)
     above = shift(down, LEN, -1)
     below = shift(upper, LEN, 1)
     inside = inner(args, halo)

time: 85.5 us -> 83.6 us (0.978)
  starting transfers between devices: 39.2 us -> 35.2 us
  waiting for transfers between devices: 21.9 us -> 24.4 us
    ppermute x0 -> x2, waiting for transfers between devices: none -> 16 us  [swap(): return lax.ppermute(x, axes, pairs + [(j, i) for i, j in pairs])]
    ppermute x0 -> x2, starting transfers between devices: none -> 14.3 us  [swap(): return lax.ppermute(x, axes, pairs + [(j, i) for i, j in pairs])]
    ppermute x5 -> x3, starting transfers between devices: 24.2 us -> 10.5 us  [shift(): return lax.ppermute(x, axes, pairs)]
    ppermute x5 -> x3, waiting for transfers between devices: 13.8 us -> 0.35 us  [shift(): return lax.ppermute(x, axes, pairs)]
    all_to_all x1, starting transfers between devices: 15 us -> 10.4 us  [total_over(): return jnp.sum(lax.all_to_all(copies, axes, 0, 0, tiled=True), axis=0)]
where the time goes in v4:
time: 83.6 us; the launch traced here: 83.3 us
  starting transfers between devices  35.2 us (42%)
  waiting for transfers between devices  24.4 us (29%)
  blocking collectives  15.1 us (18%)
  Pallas kernels  6.53 us (8%)
  between operations  0.84 us (1%)
    ppermute x2, waiting for transfers between devices, swap(): return lax.ppermute(x, axes, pairs + [(j, i) for i, j in pairs])  16 us
    all_to_all x1, blocking collectives, total_over(): return jnp.sum(lax.all_to_all(copies, axes, 0, 0, tiled=True), axis=0)  15.1 us
    ppermute x2, starting transfers between devices, swap(): return lax.ppermute(x, axes, pairs + [(j, i) for i, j in pairs])  14.3 us
    ppermute x3, starting transfers between devices, shift(): return lax.ppermute(x, axes, pairs)  10.5 us
    all_to_all x1, starting transfers between devices, total_over(): return jnp.sum(lax.all_to_all(copies, axes, 0, 0, tiled=True), axis=0)  10.4 us
    all_to_all x1, waiting for transfers between devices, total_over(): return jnp.sum(lax.all_to_all(copies, axes, 0, 0, tiled=True), axis=0)  8.06 us
    pallas_call x1, Pallas kernels, strips(): pl.pallas_call(strip_kernel, in_specs=[pl.BlockSpec(memory_space=pltpu.HB...  1.78 us
  transfers between devices with their start and end apart: 6, of which 3 were waited for; matrix products, arithmetic and copies ran while one was open for 0% of the time, Pallas kernels for 4%

profile of v4, /device:TPU:1, one launch (start us, length us, event | category | flops | bytes accessed | tf_op | source)
XLA Modules:
  0.0 83.3 jit_solution(3279760292057381358)
XLA Ops:
  0.6 0.0 copy-start.2
  0.6 0.0 copy-start.3
  0.7 0.0 copy-start.5
  0.7 0.0 copy-start.4
  0.7 0.0 copy-start
  0.7 0.0 copy-start.1
  0.7 1.8 %strips.1 = (f32[8,24,256]{2,1,0:T(8,128)S(1)}, f32[8,24,256]{2,1,0:T(8,128)S(1)}) custom-call(f32[8,32,256]{2,1,0:T(8,128)} %al.9, f32[3,8,32,256]{3,2,1,0:T(8,128)} %ve.9, s32[3,8,32,256]{3,2,1,0:T(8,128)} %up.9, s32[8,32,256]{2,1,0:T(8,128)} %ct.11, f32[8,32,256]{2,1,0:T(8,128)} %la.11, f32[8,32,256]{2,1,0:T(8,128)} %lp.9), custom_call_target="tpu_custom_call" | custom-call | tf_op jit(solution)/shard_map/strips/pallas_call | solution.py:139
  2.5 12.4 %collective-permute-start.1 = (f32[8,24,256]{2,1,0:T(8,128)S(1)}, f32[8,24,256]{2,1,0:T(8,128)S(1)}, u32[]{:S(2)}, u32[]{:S(2)}) collective-permute-start(f32[8,24,256]{2,1,0:T(8,128)S(1)} %get-tuple-element.23), channel_id=1, source_target_pairs={{0,1},{2,3},{4,5},{6,7},{1,0},{3,2},{5,4},{7,6},{8,9},{10,11},{12,... | collective-permute-start | bytes 589832 | tf_op jit(solution)/shard_map/ppermute | solution.py:48
  14.9 1.9 %collective-permute-start.2 = (f32[8,24,256]{2,1,0:T(8,128)S(1)}, f32[8,24,256]{2,1,0:T(8,128)S(1)}, u32[]{:S(2)}, u32[]{:S(2)}) collective-permute-start(f32[8,24,256]{2,1,0:T(8,128)S(1)} %get-tuple-element.24), channel_id=1, source_target_pairs={{1,2},{3,4},{5,6},{2,1},{4,3},{6,5},{9,10},{11,12},{13,14},{10,9},... | collective-permute-start | bytes 589832 | tf_op jit(solution)/shard_map/ppermute | solution.py:48
  16.8 0.0 copy-done.2
  16.9 0.0 copy-done.3
  16.9 0.0 copy-done.5
  16.9 0.0 copy-done.4
  16.9 0.0 copy-done
  16.9 0.0 copy-done.1
  16.9 0.2 early.1
  17.2 1.3 %collective-permute-start = (f32[224,256]{1,0:T(8,128)S(1)}, f32[224,256]{1,0:T(8,128)S(1)}, u32[]{:S(2)}, u32[]{:S(2)}) collective-permute-start(f32[224,256]{1,0:T(8,128)S(1)} %early.1), channel_id=1, source_target_pairs={{0,8},{8,16},{16,24},{24,32},{32,40},{40,48},{48,56},{56,64},{64,7... | collective-permute-start | bytes 688136 | tf_op jit(solution)/shard_map/ppermute | solution.py:43
  18.5 0.0 collective-permute-done.1.in_chip
  18.5 16.0 %collective-permute-done.2.off_chip = f32[8,24,256]{2,1,0:T(8,128)S(1)} collective-permute-done((f32[8,24,256]{2,1,0:T(8,128)S(1)}, f32[8,24,256]{2,1,0:T(8,128)S(1)}, u32[]{:S(2)}, u32[]{:S(2)}) %collective-permute-start.2) | collective-permute-done | bytes 196640 | tf_op jit(solution)/shard_map/ppermute | solution.py:48
  34.5 0.5 slabs.1
  35.0 1.3 %collective-permute-start.4 = (f32[176,256]{1,0:T(8,128)S(1)}, f32[176,256]{1,0:T(8,128)S(1)}, u32[]{:S(2)}, u32[]{:S(2)}) collective-permute-start(f32[176,256]{1,0:T(8,128)S(1)} %get-tuple-element.26), channel_id=1, source_target_pairs={{8,0},{16,8},{24,16},{32,24},{40,32},{48,40},{56,48},{64,56},{72,6... | collective-permute-start | bytes 540680 | tf_op jit(solution)/shard_map/ppermute | solution.py:43
  36.3 7.9 %collective-permute-start.3 = (f32[32,256]{1,0:T(8,128)S(1)}, f32[32,256]{1,0:T(8,128)S(1)}, u32[]{:S(2)}, u32[]{:S(2)}) collective-permute-start(f32[32,256]{1,0:T(8,128)S(1)} %get-tuple-element.25), channel_id=1, source_target_pairs={{0,8},{8,16},{16,24},{24,32},{32,40},{40,48},{48,56},{56,64},{64,7... | collective-permute-start | bytes 98312 | tf_op jit(solution)/shard_map/ppermute | solution.py:43
  44.2 0.0 copy-start.6
  44.2 1.3 %inner.1 = (f32[8,32,256]{2,1,0:T(8,128)S(1)}, f32[8,32,256]{2,1,0:T(8,128)S(1)}, f32[32,256]{1,0:T(8,128)S(1)}, f32[6,40,256]{2,1,0:T(8,128)S(1)}, f32[8,40,256...) custom-call(f32[8,32,256]{2,1,0:T(8,128)S(1)} %copy-done.4, ...), custom_call_target="tpu_custom_call" | custom-call | flops 20000000 | bytes 6000000 | tf_op jit(solution)/shard_map/inner/pallas_call | solution.py:427
  45.5 0.0 collective-permute-done.3.below
  45.5 0.0 collective-permute-done.raw
  45.5 0.3 collective-permute-done.4.above
  45.8 0.0 copy-done.6
  45.8 1.4 %relax.1 = (f32[8,32,256]{2,1,0:T(8,128)}, f32[8,32,256]{2,1,0:T(8,128)}, f32[32,128]{1,0:T(8,128)S(1)}) custom-call(s32[8,32,256]{2,1,0:T(8,128)S(1)} %copy-done.2, f32[8,32,256]{2,1,0:T(8,128)S(1)} %copy-done.3, s32[32,256]{1,0:T(8,128)S(1)} %copy-done.6, f32[224,256]{1,0:T(8,128)S(1)} %collective-permute-done.raw, ...), custom_call_target="tpu_custom_call" | custom-call | tf_op jit(solution)/shard_map/relax/pallas_call | solution.py:496
  47.2 15.1 %all_to_all.15 = f32[32,1,128]{2,1,0:T(1,128)S(1)} all-to-all(f32[32,1,128]{2,1,0:T(1,128)S(1)} %bitcast.4), channel_id=1, replica_groups=mesh['x'=4,'z'=12,'yh'=2,'yl'=4,'c'=2] {'x','yh','yl'}, dimensions={0} | all-to-all | bytes 32768 | tf_op jit(solution)/shard_map/all_to_all | solution.py:540
  62.3 0.1 reduce_sum.18
  62.4 0.6 broadcast_in_dim.2
  63.0 10.4 %all-to-all-start.1 = ((f32[24,1,128]{2,1,0:T(1,128)}), f32[24,1,128]{2,1,0:T(1,128)S(1)}, u32[]{:S(2)}, u32[]{:S(2)}) async-start(f32[24,1,128]{2,1,0:T(1,128)} %broadcast_in_dim.2), calls=%async_computation.1 | async-start | bytes 24576 | tf_op jit(solution)/shard_map/all_to_all | solution.py:540
  73.3 1.4 %faces.1 = f32[3,8,32,256]{3,2,1,0:T(8,128)} custom-call(f32[8,32,256]{2,1,0:T(8,128)S(1)} %copy-done.4, f32[3,8,32,256]{3,2,1,0:T(8,128)S(1)} %copy-done, s32[3,8,32,256]{3,2,1,0:T(8,128)S(1)} %copy-done.1, s32[8,32,256]{2,1,0:T(8,128)S(1)} %copy-done.2, f32[8,32,256]{2,1,0:T(8,128)S(1)} %copy-done.3, f32[8,32,256]{2,1,0:T(8,128)S(1)} %copy-done.5, ...), custom_call_target="tpu_custom_call" | custom-call | flops 5000000 | bytes 4000000 | tf_op jit(solution)/shard_map/faces/pallas_call | solution.py:530
  74.7 8.1 %all-to-all-done.1 = f32[24,1,128]{2,1,0:T(1,128)S(1)} async-done(((f32[24,1,128]{2,1,0:T(1,128)}), f32[24,1,128]{2,1,0:T(1,128)S(1)}, u32[]{:S(2)}, u32[]{:S(2)}) %all-to-all-start.1) | async-done | bytes 12320 | tf_op jit(solution)/shard_map/all_to_all | solution.py:540
  82.8 0.5 slice_multiply_fusion
  (1 shorter events, 0.0 us)
Async XLA Ops:
  0.6 16.2 %copy-start.2 = (s32[8,32,256]{2,1,0:T(8,128)S(1)}, s32[8,32,256]{2,1,0:T(8,128)}, u32[]{:S(2)}) copy-start(s32[8,32,256]{2,1,0:T(8,128)} %ct.11) | copy-start | bytes 786436
  0.6 16.2 %copy-start.3 = (f32[8,32,256]{2,1,0:T(8,128)S(1)}, f32[8,32,256]{2,1,0:T(8,128)}, u32[]{:S(2)}) copy-start(f32[8,32,256]{2,1,0:T(8,128)} %la.11) | copy-start | bytes 786436
  0.7 16.2 %copy-start.5 = (f32[8,32,256]{2,1,0:T(8,128)S(1)}, f32[8,32,256]{2,1,0:T(8,128)}, u32[]{:S(2)}) copy-start(f32[8,32,256]{2,1,0:T(8,128)} %lp.9) | copy-start | bytes 786436
  0.7 16.2 %copy-start.4 = (f32[8,32,256]{2,1,0:T(8,128)S(1)}, f32[8,32,256]{2,1,0:T(8,128)}, u32[]{:S(2)}) copy-start(f32[8,32,256]{2,1,0:T(8,128)} %al.9) | copy-start | bytes 786436
  0.7 16.2 %copy-start = (f32[3,8,32,256]{3,2,1,0:T(8,128)S(1)}, f32[3,8,32,256]{3,2,1,0:T(8,128)}, u32[]{:S(2)}) copy-start(f32[3,8,32,256]{3,2,1,0:T(8,128)} %ve.9) | copy-start | bytes 2359300
  0.7 16.2 %copy-start.1 = (s32[3,8,32,256]{3,2,1,0:T(8,128)S(1)}, s32[3,8,32,256]{3,2,1,0:T(8,128)}, u32[]{:S(2)}) copy-start(s32[3,8,32,256]{3,2,1,0:T(8,128)} %up.9) | copy-start | bytes 2359300
  2.5 16.0 %collective-permute-start.1 = (f32[8,24,256]{2,1,0:T(8,128)S(1)}, f32[8,24,256]{2,1,0:T(8,128)S(1)}, u32[]{:S(2)}, u32[]{:S(2)}) collective-permute-start(f32[8,24,256]{2,1,0:T(8,128)S(1)} %get-tuple-element.23), channel_id=1, source_target_pairs={{0,1},{2,3},{4,5},{6,7},{1,0},{3,2},{5,4},{7,6},{8,9},{10,11},{12,... | collective-permute-start | bytes 589832 | tf_op jit(solution)/shard_map/ppermute | solution.py:48
  14.9 19.6 %collective-permute-start.2 = (f32[8,24,256]{2,1,0:T(8,128)S(1)}, f32[8,24,256]{2,1,0:T(8,128)S(1)}, u32[]{:S(2)}, u32[]{:S(2)}) collective-permute-start(f32[8,24,256]{2,1,0:T(8,128)S(1)} %get-tuple-element.24), channel_id=1, source_target_pairs={{1,2},{3,4},{5,6},{2,1},{4,3},{6,5},{9,10},{11,12},{13,14},{10,9},... | collective-permute-start | bytes 589832 | tf_op jit(solution)/shard_map/ppermute | solution.py:48
  17.2 28.3 %collective-permute-start = (f32[224,256]{1,0:T(8,128)S(1)}, f32[224,256]{1,0:T(8,128)S(1)}, u32[]{:S(2)}, u32[]{:S(2)}) collective-permute-start(f32[224,256]{1,0:T(8,128)S(1)} %early.1), channel_id=1, source_target_pairs={{0,8},{8,16},{16,24},{24,32},{32,40},{40,48},{48,56},{56,64},{64,7... | collective-permute-start | bytes 688136 | tf_op jit(solution)/shard_map/ppermute | solution.py:43
  35.0 10.8 %collective-permute-start.4 = (f32[176,256]{1,0:T(8,128)S(1)}, f32[176,256]{1,0:T(8,128)S(1)}, u32[]{:S(2)}, u32[]{:S(2)}) collective-permute-start(f32[176,256]{1,0:T(8,128)S(1)} %get-tuple-element.26), channel_id=1, source_target_pairs={{8,0},{16,8},{24,16},{32,24},{40,32},{48,40},{56,48},{64,56},{72,6... | collective-permute-start | bytes 540680 | tf_op jit(solution)/shard_map/ppermute | solution.py:43
  36.3 9.2 %collective-permute-start.3 = (f32[32,256]{1,0:T(8,128)S(1)}, f32[32,256]{1,0:T(8,128)S(1)}, u32[]{:S(2)}, u32[]{:S(2)}) collective-permute-start(f32[32,256]{1,0:T(8,128)S(1)} %get-tuple-element.25), channel_id=1, source_target_pairs={{0,8},{8,16},{16,24},{24,32},{32,40},{40,48},{48,56},{56,64},{64,7... | collective-permute-start | bytes 98312 | tf_op jit(solution)/shard_map/ppermute | solution.py:43
  44.2 1.6 %copy-start.6 = (s32[32,256]{1,0:T(8,128)S(1)}, s32[32,256]{1,0:T(8,128)}, u32[]{:S(2)}) copy-start(s32[32,256]{1,0:T(8,128)} %ow.1) | copy-start | bytes 98308
  63.0 19.8 %all-to-all-start.1 = ((f32[24,1,128]{2,1,0:T(1,128)}), f32[24,1,128]{2,1,0:T(1,128)S(1)}, u32[]{:S(2)}, u32[]{:S(2)}) async-start(f32[24,1,128]{2,1,0:T(1,128)} %broadcast_in_dim.2), calls=%async_computation.1 | async-start | bytes 24576 | tf_op jit(solution)/shard_map/all_to_all | solution.py:540

commit v5 on v4

--- a/solution.py
+++ b/solution.py
@@ -13,8 +13,8 @@
 PORTS = 16
 LEN = ("x", "z", "yh")
 XS = ("yl", "c")
-FIRST = ("x", "yh", "yl")
-SECOND = ("z", "c")
+FIRST = ("z", "c")
+SECOND = ("x", "yh", "yl")
 SIZES = {"x": 4, "z": 12, "yh": 2, "yl": 4, "c": 2}
 PLANES = 8
 ROWS = 32

time: 83.6 us -> 82.2 us (0.983)
  blocking collectives: 15.1 us -> 12.1 us
  starting transfers between devices: 35.2 us -> 37.5 us
    all_to_all x1, blocking collectives: 15.1 us -> 12.1 us  [total_over(): return jnp.sum(lax.all_to_all(copies, axes, 0, 0, tiled=True), axis=0)]
    all_to_all x1, starting transfers between devices: 10.4 us -> 12.7 us  [total_over(): return jnp.sum(lax.all_to_all(copies, axes, 0, 0, tiled=True), axis=0)]
where the time goes in v5:
time: 82.2 us; the launch traced here: 81.9 us
  starting transfers between devices  37.5 us (46%)
  waiting for transfers between devices  23.6 us (29%)
  blocking collectives  12.1 us (15%)
  Pallas kernels  6.54 us (8%)
  between operations  0.84 us (1%)
    ppermute x2, waiting for transfers between devices, swap(): return lax.ppermute(x, axes, pairs + [(j, i) for i, j in pairs])  16 us
    ppermute x2, starting transfers between devices, swap(): return lax.ppermute(x, axes, pairs + [(j, i) for i, j in pairs])  14.3 us
    all_to_all x1, starting transfers between devices, total_over(): return jnp.sum(lax.all_to_all(copies, axes, 0, 0, tiled=True), axis=0)  12.7 us
    all_to_all x1, blocking collectives, total_over(): return jnp.sum(lax.all_to_all(copies, axes, 0, 0, tiled=True), axis=0)  12.1 us
    ppermute x3, starting transfers between devices, shift(): return lax.ppermute(x, axes, pairs)  10.5 us
    all_to_all x1, waiting for transfers between devices, total_over(): return jnp.sum(lax.all_to_all(copies, axes, 0, 0, tiled=True), axis=0)  7.28 us
    pallas_call x1, Pallas kernels, strips(): pl.pallas_call(strip_kernel, in_specs=[pl.BlockSpec(memory_space=pltpu.HB...  1.78 us
  transfers between devices with their start and end apart: 6, of which 3 were waited for; matrix products, arithmetic and copies ran while one was open for 0% of the time, Pallas kernels for 4%

profile of v5, /device:TPU:1, one launch (start us, length us, event | category | flops | bytes accessed | tf_op | source)
XLA Modules:
  0.0 81.9 jit_solution(7748321339978007702)
XLA Ops:
  0.6 0.0 copy-start.2
  0.6 0.0 copy-start.3
  0.7 0.0 copy-start.5
  0.7 0.0 copy-start.4
  0.7 0.0 copy-start
  0.7 0.0 copy-start.1
  0.7 1.8 %strips.1 = (f32[8,24,256]{2,1,0:T(8,128)S(1)}, f32[8,24,256]{2,1,0:T(8,128)S(1)}) custom-call(f32[8,32,256]{2,1,0:T(8,128)} %al.9, f32[3,8,32,256]{3,2,1,0:T(8,128)} %ve.9, s32[3,8,32,256]{3,2,1,0:T(8,128)} %up.9, s32[8,32,256]{2,1,0:T(8,128)} %ct.11, f32[8,32,256]{2,1,0:T(8,128)} %la.11, f32[8,32,256]{2,1,0:T(8,128)} %lp.9), custom_call_target="tpu_custom_call" | custom-call | tf_op jit(solution)/shard_map/strips/pallas_call | solution.py:139
  2.5 12.4 %collective-permute-start.1 = (f32[8,24,256]{2,1,0:T(8,128)S(1)}, f32[8,24,256]{2,1,0:T(8,128)S(1)}, u32[]{:S(2)}, u32[]{:S(2)}) collective-permute-start(f32[8,24,256]{2,1,0:T(8,128)S(1)} %get-tuple-element.23), channel_id=1, source_target_pairs={{0,1},{2,3},{4,5},{6,7},{1,0},{3,2},{5,4},{7,6},{8,9},{10,11},{12,... | collective-permute-start | bytes 589832 | tf_op jit(solution)/shard_map/ppermute | solution.py:48
  14.9 1.9 %collective-permute-start.2 = (f32[8,24,256]{2,1,0:T(8,128)S(1)}, f32[8,24,256]{2,1,0:T(8,128)S(1)}, u32[]{:S(2)}, u32[]{:S(2)}) collective-permute-start(f32[8,24,256]{2,1,0:T(8,128)S(1)} %get-tuple-element.24), channel_id=1, source_target_pairs={{1,2},{3,4},{5,6},{2,1},{4,3},{6,5},{9,10},{11,12},{13,14},{10,9},... | collective-permute-start | bytes 589832 | tf_op jit(solution)/shard_map/ppermute | solution.py:48
  16.8 0.0 copy-done.2
  16.9 0.0 copy-done.3
  16.9 0.0 copy-done.5
  16.9 0.0 copy-done.4
  16.9 0.0 copy-done
  16.9 0.0 copy-done.1
  16.9 0.2 early.1
  17.2 1.3 %collective-permute-start = (f32[224,256]{1,0:T(8,128)S(1)}, f32[224,256]{1,0:T(8,128)S(1)}, u32[]{:S(2)}, u32[]{:S(2)}) collective-permute-start(f32[224,256]{1,0:T(8,128)S(1)} %early.1), channel_id=1, source_target_pairs={{0,8},{8,16},{16,24},{24,32},{32,40},{40,48},{48,56},{56,64},{64,7... | collective-permute-start | bytes 688136 | tf_op jit(solution)/shard_map/ppermute | solution.py:43
  18.5 0.0 collective-permute-done.1.in_chip
  18.5 16.0 %collective-permute-done.2.off_chip = f32[8,24,256]{2,1,0:T(8,128)S(1)} collective-permute-done((f32[8,24,256]{2,1,0:T(8,128)S(1)}, f32[8,24,256]{2,1,0:T(8,128)S(1)}, u32[]{:S(2)}, u32[]{:S(2)}) %collective-permute-start.2) | collective-permute-done | bytes 196640 | tf_op jit(solution)/shard_map/ppermute | solution.py:48
  34.5 0.5 slabs.1
  35.0 1.3 %collective-permute-start.4 = (f32[176,256]{1,0:T(8,128)S(1)}, f32[176,256]{1,0:T(8,128)S(1)}, u32[]{:S(2)}, u32[]{:S(2)}) collective-permute-start(f32[176,256]{1,0:T(8,128)S(1)} %get-tuple-element.26), channel_id=1, source_target_pairs={{8,0},{16,8},{24,16},{32,24},{40,32},{48,40},{56,48},{64,56},{72,6... | collective-permute-start | bytes 540680 | tf_op jit(solution)/shard_map/ppermute | solution.py:43
  36.3 7.9 %collective-permute-start.3 = (f32[32,256]{1,0:T(8,128)S(1)}, f32[32,256]{1,0:T(8,128)S(1)}, u32[]{:S(2)}, u32[]{:S(2)}) collective-permute-start(f32[32,256]{1,0:T(8,128)S(1)} %get-tuple-element.25), channel_id=1, source_target_pairs={{0,8},{8,16},{16,24},{24,32},{32,40},{40,48},{48,56},{56,64},{64,7... | collective-permute-start | bytes 98312 | tf_op jit(solution)/shard_map/ppermute | solution.py:43
  44.2 0.0 copy-start.6
  44.2 1.3 %inner.1 = (f32[8,32,256]{2,1,0:T(8,128)S(1)}, f32[8,32,256]{2,1,0:T(8,128)S(1)}, f32[32,256]{1,0:T(8,128)S(1)}, f32[6,40,256]{2,1,0:T(8,128)S(1)}, f32[8,40,256...) custom-call(f32[8,32,256]{2,1,0:T(8,128)S(1)} %copy-done.4, ...), custom_call_target="tpu_custom_call" | custom-call | flops 20000000 | bytes 6000000 | tf_op jit(solution)/shard_map/inner/pallas_call | solution.py:427
  45.5 0.0 collective-permute-done.3.below
  45.5 0.0 collective-permute-done.raw
  45.5 0.3 collective-permute-done.4.above
  45.8 0.0 copy-done.6
  45.8 1.4 %relax.1 = (f32[8,32,256]{2,1,0:T(8,128)}, f32[8,32,256]{2,1,0:T(8,128)}, f32[24,128]{1,0:T(8,128)S(1)}) custom-call(s32[8,32,256]{2,1,0:T(8,128)S(1)} %copy-done.2, f32[8,32,256]{2,1,0:T(8,128)S(1)} %copy-done.3, s32[32,256]{1,0:T(8,128)S(1)} %copy-done.6, f32[224,256]{1,0:T(8,128)S(1)} %collective-permute-done.raw, ...), custom_call_target="tpu_custom_call" | custom-call | tf_op jit(solution)/shard_map/relax/pallas_call | solution.py:496
  47.2 12.1 %all_to_all.15 = f32[24,1,128]{2,1,0:T(1,128)S(1)} all-to-all(f32[24,1,128]{2,1,0:T(1,128)S(1)} %bitcast.4), channel_id=1, replica_groups=mesh['x'=4,'z'=12,'yh'=2,'yl'=4,'c'=2] {'z','c'}, dimensions={0} | all-to-all | bytes 24576 | tf_op jit(solution)/shard_map/all_to_all | solution.py:540
  59.4 0.6 broadcast_in_dim.2
  60.0 12.7 %all-to-all-start.1 = ((f32[32,1,128]{2,1,0:T(1,128)}), f32[32,1,128]{2,1,0:T(1,128)S(1)}, u32[]{:S(2)}, u32[]{:S(2)}) async-start(f32[32,1,128]{2,1,0:T(1,128)} %broadcast_in_dim.2), calls=%async_computation.1 | async-start | bytes 32768 | tf_op jit(solution)/shard_map/all_to_all | solution.py:540
  72.7 1.4 %faces.1 = f32[3,8,32,256]{3,2,1,0:T(8,128)} custom-call(f32[8,32,256]{2,1,0:T(8,128)S(1)} %copy-done.4, f32[3,8,32,256]{3,2,1,0:T(8,128)S(1)} %copy-done, s32[3,8,32,256]{3,2,1,0:T(8,128)S(1)} %copy-done.1, s32[8,32,256]{2,1,0:T(8,128)S(1)} %copy-done.2, f32[8,32,256]{2,1,0:T(8,128)S(1)} %copy-done.3, f32[8,32,256]{2,1,0:T(8,128)S(1)} %copy-done.5, ...), custom_call_target="tpu_custom_call" | custom-call | flops 5000000 | bytes 4000000 | tf_op jit(solution)/shard_map/faces/pallas_call | solution.py:530
  74.0 7.3 %all-to-all-done.1 = f32[32,1,128]{2,1,0:T(1,128)S(1)} async-done(((f32[32,1,128]{2,1,0:T(1,128)}), f32[32,1,128]{2,1,0:T(1,128)S(1)}, u32[]{:S(2)}, u32[]{:S(2)}) %all-to-all-start.1) | async-done | bytes 16416 | tf_op jit(solution)/shard_map/all_to_all | solution.py:540
  81.3 0.5 slice_multiply_fusion
  (2 shorter events, 0.1 us)
Async XLA Ops:
  0.6 16.2 %copy-start.2 = (s32[8,32,256]{2,1,0:T(8,128)S(1)}, s32[8,32,256]{2,1,0:T(8,128)}, u32[]{:S(2)}) copy-start(s32[8,32,256]{2,1,0:T(8,128)} %ct.11) | copy-start | bytes 786436
  0.6 16.2 %copy-start.3 = (f32[8,32,256]{2,1,0:T(8,128)S(1)}, f32[8,32,256]{2,1,0:T(8,128)}, u32[]{:S(2)}) copy-start(f32[8,32,256]{2,1,0:T(8,128)} %la.11) | copy-start | bytes 786436
  0.7 16.2 %copy-start.5 = (f32[8,32,256]{2,1,0:T(8,128)S(1)}, f32[8,32,256]{2,1,0:T(8,128)}, u32[]{:S(2)}) copy-start(f32[8,32,256]{2,1,0:T(8,128)} %lp.9) | copy-start | bytes 786436
  0.7 16.2 %copy-start.4 = (f32[8,32,256]{2,1,0:T(8,128)S(1)}, f32[8,32,256]{2,1,0:T(8,128)}, u32[]{:S(2)}) copy-start(f32[8,32,256]{2,1,0:T(8,128)} %al.9) | copy-start | bytes 786436
  0.7 16.2 %copy-start = (f32[3,8,32,256]{3,2,1,0:T(8,128)S(1)}, f32[3,8,32,256]{3,2,1,0:T(8,128)}, u32[]{:S(2)}) copy-start(f32[3,8,32,256]{3,2,1,0:T(8,128)} %ve.9) | copy-start | bytes 2359300
  0.7 16.2 %copy-start.1 = (s32[3,8,32,256]{3,2,1,0:T(8,128)S(1)}, s32[3,8,32,256]{3,2,1,0:T(8,128)}, u32[]{:S(2)}) copy-start(s32[3,8,32,256]{3,2,1,0:T(8,128)} %up.9) | copy-start | bytes 2359300
  2.5 16.0 %collective-permute-start.1 = (f32[8,24,256]{2,1,0:T(8,128)S(1)}, f32[8,24,256]{2,1,0:T(8,128)S(1)}, u32[]{:S(2)}, u32[]{:S(2)}) collective-permute-start(f32[8,24,256]{2,1,0:T(8,128)S(1)} %get-tuple-element.23), channel_id=1, source_target_pairs={{0,1},{2,3},{4,5},{6,7},{1,0},{3,2},{5,4},{7,6},{8,9},{10,11},{12,... | collective-permute-start | bytes 589832 | tf_op jit(solution)/shard_map/ppermute | solution.py:48
  14.9 19.6 %collective-permute-start.2 = (f32[8,24,256]{2,1,0:T(8,128)S(1)}, f32[8,24,256]{2,1,0:T(8,128)S(1)}, u32[]{:S(2)}, u32[]{:S(2)}) collective-permute-start(f32[8,24,256]{2,1,0:T(8,128)S(1)} %get-tuple-element.24), channel_id=1, source_target_pairs={{1,2},{3,4},{5,6},{2,1},{4,3},{6,5},{9,10},{11,12},{13,14},{10,9},... | collective-permute-start | bytes 589832 | tf_op jit(solution)/shard_map/ppermute | solution.py:48
  17.2 28.3 %collective-permute-start = (f32[224,256]{1,0:T(8,128)S(1)}, f32[224,256]{1,0:T(8,128)S(1)}, u32[]{:S(2)}, u32[]{:S(2)}) collective-permute-start(f32[224,256]{1,0:T(8,128)S(1)} %early.1), channel_id=1, source_target_pairs={{0,8},{8,16},{16,24},{24,32},{32,40},{40,48},{48,56},{56,64},{64,7... | collective-permute-start | bytes 688136 | tf_op jit(solution)/shard_map/ppermute | solution.py:43
  35.0 10.8 %collective-permute-start.4 = (f32[176,256]{1,0:T(8,128)S(1)}, f32[176,256]{1,0:T(8,128)S(1)}, u32[]{:S(2)}, u32[]{:S(2)}) collective-permute-start(f32[176,256]{1,0:T(8,128)S(1)} %get-tuple-element.26), channel_id=1, source_target_pairs={{8,0},{16,8},{24,16},{32,24},{40,32},{48,40},{56,48},{64,56},{72,6... | collective-permute-start | bytes 540680 | tf_op jit(solution)/shard_map/ppermute | solution.py:43
  36.3 9.2 %collective-permute-start.3 = (f32[32,256]{1,0:T(8,128)S(1)}, f32[32,256]{1,0:T(8,128)S(1)}, u32[]{:S(2)}, u32[]{:S(2)}) collective-permute-start(f32[32,256]{1,0:T(8,128)S(1)} %get-tuple-element.25), channel_id=1, source_target_pairs={{0,8},{8,16},{16,24},{24,32},{32,40},{40,48},{48,56},{56,64},{64,7... | collective-permute-start | bytes 98312 | tf_op jit(solution)/shard_map/ppermute | solution.py:43
  44.2 1.6 %copy-start.6 = (s32[32,256]{1,0:T(8,128)S(1)}, s32[32,256]{1,0:T(8,128)}, u32[]{:S(2)}) copy-start(s32[32,256]{1,0:T(8,128)} %ow.1) | copy-start | bytes 98308
  60.0 21.3 %all-to-all-start.1 = ((f32[32,1,128]{2,1,0:T(1,128)}), f32[32,1,128]{2,1,0:T(1,128)S(1)}, u32[]{:S(2)}, u32[]{:S(2)}) async-start(f32[32,1,128]{2,1,0:T(1,128)} %broadcast_in_dim.2), calls=%async_computation.1 | async-start | bytes 32768 | tf_op jit(solution)/shard_map/all_to_all | solution.py:540

commit v6 on v5

--- a/solution.py
+++ b/solution.py
@@ -96,7 +96,7 @@
     return lax.broadcasted_iota(jnp.int32, shape, 0)
 
 
-def strip_kernel(al, ve, up, ct, la, lp, in_chip, off_chip, *scratch):
+def strip_kernel(al, ve, up, ct, la, lp, off_chip, in_chip, *scratch):
     sem = scratch[-1]
     last, first = scratch[:6], scratch[6:12]
     copies = []
@@ -292,7 +292,7 @@
     return jnp.where(sublanes((HALO, NZ)) == 0, plane[:HALO], plane[ROWS - HALO : ROWS])
 
 
-def slab_kernel(al, ve, up, ct, la, lp, in_chip, off_chip, halo, down, upper):
+def slab_kernel(al, ve, up, ct, la, lp, off_chip, in_chip, halo, down, upper):
     fill_halo(in_chip, off_chip, halo)
     own = Own(al, ve, up, ct, la, lp, halo)
     top = PLANES - 1
@@ -542,11 +542,11 @@
 
 def body(alpha, velocity, upwind, celltype, owner, lam_alpha, lam_press):
     args = (alpha, velocity, upwind, celltype, lam_alpha, lam_press)
-    in_chip, off_chip = strips(*args)
+    off_chip, in_chip = strips(*args)
+    off_chip = swap(off_chip, XS, 1)
     in_chip = swap(in_chip, XS, 0)
-    off_chip = swap(off_chip, XS, 1)
     raw = shift(early(*args), LEN, 1)
-    halo, down, upper = slabs(*args, in_chip, off_chip)
+    halo, down, upper = slabs(*args, off_chip, in_chip)
     above = shift(down, LEN, -1)
     below = shift(upper, LEN, 1)
     inside = inner(args, halo)

time: 82.2 us -> 83.1 us (1.011)
  blocking collectives: 12.1 us -> 19.4 us
  starting transfers between devices: 37.5 us -> 33.9 us
  waiting for transfers between devices: 23.6 us -> 20.9 us
    ppermute x2, waiting for transfers between devices: 16 us -> 0.01 us  [swap(): return lax.ppermute(x, axes, pairs + [(j, i) for i, j in pairs])]
    ppermute x3, waiting for transfers between devices: 0.34 us -> 13.7 us  [shift(): return lax.ppermute(x, axes, pairs)]
    all_to_all x1, blocking collectives: 12.1 us -> 19.4 us  [total_over(): return jnp.sum(lax.all_to_all(copies, axes, 0, 0, tiled=True), axis=0)]
    all_to_all x1, starting transfers between devices: 12.7 us -> 10.3 us  [total_over(): return jnp.sum(lax.all_to_all(copies, axes, 0, 0, tiled=True), axis=0)]
    ppermute x2, starting transfers between devices: 14.3 us -> 13.1 us  [swap(): return lax.ppermute(x, axes, pairs + [(j, i) for i, j in pairs])]
where the time goes in v6:
time: 83.1 us; the launch traced here: 82.8 us
  starting transfers between devices  33.9 us (41%)
  waiting for transfers between devices  20.9 us (25%)
  blocking collectives  19.4 us (23%)
  Pallas kernels  6.55 us (8%)
    all_to_all x1, blocking collectives, total_over(): return jnp.sum(lax.all_to_all(copies, axes, 0, 0, tiled=True), axis=0)  19.4 us
    ppermute x3, waiting for transfers between devices, shift(): return lax.ppermute(x, axes, pairs)  13.7 us
    ppermute x2, starting transfers between devices, swap(): return lax.ppermute(x, axes, pairs + [(j, i) for i, j in pairs])  13.1 us
    ppermute x3, starting transfers between devices, shift(): return lax.ppermute(x, axes, pairs)  10.5 us
    all_to_all x1, starting transfers between devices, total_over(): return jnp.sum(lax.all_to_all(copies, axes, 0, 0, tiled=True), axis=0)  10.3 us
    all_to_all x1, waiting for transfers between devices, total_over(): return jnp.sum(lax.all_to_all(copies, axes, 0, 0, tiled=True), axis=0)  7.28 us
    pallas_call x1, Pallas kernels, strips(): pl.pallas_call(strip_kernel, in_specs=[pl.BlockSpec(memory_space=pltpu.HB...  1.78 us
  transfers between devices with their start and end apart: 6, of which 3 were waited for; matrix products, arithmetic and copies ran while one was open for 0% of the time, Pallas kernels for 4%

profile of v6, /device:TPU:1, one launch (start us, length us, event | category | flops | bytes accessed | tf_op | source)
XLA Modules:
  0.0 82.8 jit_solution(14182168961831945252)
XLA Ops:
  0.6 0.0 copy-start.2
  0.6 0.0 copy-start.3
  0.7 0.0 copy-start.5
  0.7 0.0 copy-start.4
  0.7 0.0 copy-start
  0.7 0.0 copy-start.1
  0.7 1.8 %strips.1 = (f32[8,24,256]{2,1,0:T(8,128)S(1)}, f32[8,24,256]{2,1,0:T(8,128)S(1)}) custom-call(f32[8,32,256]{2,1,0:T(8,128)} %al.9, f32[3,8,32,256]{3,2,1,0:T(8,128)} %ve.9, s32[3,8,32,256]{3,2,1,0:T(8,128)} %up.9, s32[8,32,256]{2,1,0:T(8,128)} %ct.11, f32[8,32,256]{2,1,0:T(8,128)} %la.11, f32[8,32,256]{2,1,0:T(8,128)} %lp.9), custom_call_target="tpu_custom_call" | custom-call | tf_op jit(solution)/shard_map/strips/pallas_call | solution.py:139
  2.5 4.6 %collective-permute-start.1 = (f32[8,24,256]{2,1,0:T(8,128)S(1)}, f32[8,24,256]{2,1,0:T(8,128)S(1)}, u32[]{:S(2)}, u32[]{:S(2)}) collective-permute-start(f32[8,24,256]{2,1,0:T(8,128)S(1)} %get-tuple-element.23), channel_id=1, source_target_pairs={{1,2},{3,4},{5,6},{2,1},{4,3},{6,5},{9,10},{11,12},{13,14},{10,9},... | collective-permute-start | bytes 589832 | tf_op jit(solution)/shard_map/ppermute | solution.py:48
  7.1 8.5 %collective-permute-start.2 = (f32[8,24,256]{2,1,0:T(8,128)S(1)}, f32[8,24,256]{2,1,0:T(8,128)S(1)}, u32[]{:S(2)}, u32[]{:S(2)}) collective-permute-start(f32[8,24,256]{2,1,0:T(8,128)S(1)} %get-tuple-element.24), channel_id=1, source_target_pairs={{0,1},{2,3},{4,5},{6,7},{1,0},{3,2},{5,4},{7,6},{8,9},{10,11},{12,... | collective-permute-start | bytes 589832 | tf_op jit(solution)/shard_map/ppermute | solution.py:48
  15.6 0.0 copy-done.2
  15.6 0.0 copy-done.3
  15.6 0.0 copy-done.5
  15.6 0.0 copy-done.4
  15.6 0.0 copy-done
  15.6 0.0 copy-done.1
  15.7 0.2 early.1
  15.9 1.3 %collective-permute-start = (f32[224,256]{1,0:T(8,128)S(1)}, f32[224,256]{1,0:T(8,128)S(1)}, u32[]{:S(2)}, u32[]{:S(2)}) collective-permute-start(f32[224,256]{1,0:T(8,128)S(1)} %early.1), channel_id=1, source_target_pairs={{0,8},{8,16},{16,24},{24,32},{32,40},{40,48},{48,56},{56,64},{64,7... | collective-permute-start | bytes 688136 | tf_op jit(solution)/shard_map/ppermute | solution.py:43
  17.2 0.0 collective-permute-done.1.off_chip
  17.2 0.0 collective-permute-done.2.in_chip
  17.2 0.5 slabs.1
  17.8 1.3 %collective-permute-start.4 = (f32[176,256]{1,0:T(8,128)S(1)}, f32[176,256]{1,0:T(8,128)S(1)}, u32[]{:S(2)}, u32[]{:S(2)}) collective-permute-start(f32[176,256]{1,0:T(8,128)S(1)} %get-tuple-element.26), channel_id=1, source_target_pairs={{8,0},{16,8},{24,16},{32,24},{40,32},{48,40},{56,48},{64,56},{72,6... | collective-permute-start | bytes 540680 | tf_op jit(solution)/shard_map/ppermute | solution.py:43
  19.1 7.9 %collective-permute-start.3 = (f32[32,256]{1,0:T(8,128)S(1)}, f32[32,256]{1,0:T(8,128)S(1)}, u32[]{:S(2)}, u32[]{:S(2)}) collective-permute-start(f32[32,256]{1,0:T(8,128)S(1)} %get-tuple-element.25), channel_id=1, source_target_pairs={{0,8},{8,16},{16,24},{24,32},{32,40},{40,48},{48,56},{56,64},{64,7... | collective-permute-start | bytes 98312 | tf_op jit(solution)/shard_map/ppermute | solution.py:43
  27.0 0.0 copy-start.6
  27.0 1.3 %inner.1 = (f32[8,32,256]{2,1,0:T(8,128)S(1)}, f32[8,32,256]{2,1,0:T(8,128)S(1)}, f32[32,256]{1,0:T(8,128)S(1)}, f32[6,40,256]{2,1,0:T(8,128)S(1)}, f32[8,40,256...) custom-call(f32[8,32,256]{2,1,0:T(8,128)S(1)} %copy-done.4, ...), custom_call_target="tpu_custom_call" | custom-call | flops 20000000 | bytes 6000000 | tf_op jit(solution)/shard_map/inner/pallas_call | solution.py:427
  28.2 3.3 %collective-permute-done.3.below = f32[32,256]{1,0:T(8,128)S(1)} collective-permute-done((f32[32,256]{1,0:T(8,128)S(1)}, f32[32,256]{1,0:T(8,128)S(1)}, u32[]{:S(2)}, u32[]{:S(2)}) %collective-permute-start.3) | collective-permute-done | bytes 32800 | tf_op jit(solution)/shard_map/ppermute | solution.py:43
  31.6 0.0 collective-permute-done.raw
  31.6 10.3 %collective-permute-done.4.above = f32[176,256]{1,0:T(8,128)S(1)} collective-permute-done((f32[176,256]{1,0:T(8,128)S(1)}, f32[176,256]{1,0:T(8,128)S(1)}, u32[]{:S(2)}, u32[]{:S(2)}) %collective-permute-start.4) | collective-permute-done | bytes 180256 | tf_op jit(solution)/shard_map/ppermute | solution.py:43
  41.9 0.0 copy-done.6
  41.9 1.4 %relax.1 = (f32[8,32,256]{2,1,0:T(8,128)}, f32[8,32,256]{2,1,0:T(8,128)}, f32[24,128]{1,0:T(8,128)S(1)}) custom-call(s32[8,32,256]{2,1,0:T(8,128)S(1)} %copy-done.2, f32[8,32,256]{2,1,0:T(8,128)S(1)} %copy-done.3, s32[32,256]{1,0:T(8,128)S(1)} %copy-done.6, f32[224,256]{1,0:T(8,128)S(1)} %collective-permute-done.raw, ...), custom_call_target="tpu_custom_call" | custom-call | tf_op jit(solution)/shard_map/relax/pallas_call | solution.py:496
  43.3 19.4 %all_to_all.15 = f32[24,1,128]{2,1,0:T(1,128)S(1)} all-to-all(f32[24,1,128]{2,1,0:T(1,128)S(1)} %bitcast.4), channel_id=1, replica_groups=mesh['x'=4,'z'=12,'yh'=2,'yl'=4,'c'=2] {'z','c'}, dimensions={0} | all-to-all | bytes 24576 | tf_op jit(solution)/shard_map/all_to_all | solution.py:540
  62.7 0.6 broadcast_in_dim.2
  63.4 10.3 %all-to-all-start.1 = ((f32[32,1,128]{2,1,0:T(1,128)}), f32[32,1,128]{2,1,0:T(1,128)S(1)}, u32[]{:S(2)}, u32[]{:S(2)}) async-start(f32[32,1,128]{2,1,0:T(1,128)} %broadcast_in_dim.2), calls=%async_computation.1 | async-start | bytes 32768 | tf_op jit(solution)/shard_map/all_to_all | solution.py:540
  73.7 1.4 %faces.1 = f32[3,8,32,256]{3,2,1,0:T(8,128)} custom-call(f32[8,32,256]{2,1,0:T(8,128)S(1)} %copy-done.4, f32[3,8,32,256]{3,2,1,0:T(8,128)S(1)} %copy-done, s32[3,8,32,256]{3,2,1,0:T(8,128)S(1)} %copy-done.1, s32[8,32,256]{2,1,0:T(8,128)S(1)} %copy-done.2, f32[8,32,256]{2,1,0:T(8,128)S(1)} %copy-done.3, f32[8,32,256]{2,1,0:T(8,128)S(1)} %copy-done.5, ...), custom_call_target="tpu_custom_call" | custom-call | flops 5000000 | bytes 4000000 | tf_op jit(solution)/shard_map/faces/pallas_call | solution.py:530
  75.0 7.3 %all-to-all-done.1 = f32[32,1,128]{2,1,0:T(1,128)S(1)} async-done(((f32[32,1,128]{2,1,0:T(1,128)}), f32[32,1,128]{2,1,0:T(1,128)S(1)}, u32[]{:S(2)}, u32[]{:S(2)}) %all-to-all-start.1) | async-done | bytes 16416 | tf_op jit(solution)/shard_map/all_to_all | solution.py:540
  82.3 0.5 slice_multiply_fusion
  (2 shorter events, 0.1 us)
Async XLA Ops:
  0.6 15.0 %copy-start.2 = (s32[8,32,256]{2,1,0:T(8,128)S(1)}, s32[8,32,256]{2,1,0:T(8,128)}, u32[]{:S(2)}) copy-start(s32[8,32,256]{2,1,0:T(8,128)} %ct.11) | copy-start | bytes 786436
  0.6 15.0 %copy-start.3 = (f32[8,32,256]{2,1,0:T(8,128)S(1)}, f32[8,32,256]{2,1,0:T(8,128)}, u32[]{:S(2)}) copy-start(f32[8,32,256]{2,1,0:T(8,128)} %la.11) | copy-start | bytes 786436
  0.7 15.0 %copy-start.5 = (f32[8,32,256]{2,1,0:T(8,128)S(1)}, f32[8,32,256]{2,1,0:T(8,128)}, u32[]{:S(2)}) copy-start(f32[8,32,256]{2,1,0:T(8,128)} %lp.9) | copy-start | bytes 786436
  0.7 15.0 %copy-start.4 = (f32[8,32,256]{2,1,0:T(8,128)S(1)}, f32[8,32,256]{2,1,0:T(8,128)}, u32[]{:S(2)}) copy-start(f32[8,32,256]{2,1,0:T(8,128)} %al.9) | copy-start | bytes 786436
  0.7 15.0 %copy-start = (f32[3,8,32,256]{3,2,1,0:T(8,128)S(1)}, f32[3,8,32,256]{3,2,1,0:T(8,128)}, u32[]{:S(2)}) copy-start(f32[3,8,32,256]{3,2,1,0:T(8,128)} %ve.9) | copy-start | bytes 2359300
  0.7 15.0 %copy-start.1 = (s32[3,8,32,256]{3,2,1,0:T(8,128)S(1)}, s32[3,8,32,256]{3,2,1,0:T(8,128)}, u32[]{:S(2)}) copy-start(s32[3,8,32,256]{3,2,1,0:T(8,128)} %up.9) | copy-start | bytes 2359300
  2.5 14.7 %collective-permute-start.1 = (f32[8,24,256]{2,1,0:T(8,128)S(1)}, f32[8,24,256]{2,1,0:T(8,128)S(1)}, u32[]{:S(2)}, u32[]{:S(2)}) collective-permute-start(f32[8,24,256]{2,1,0:T(8,128)S(1)} %get-tuple-element.23), channel_id=1, source_target_pairs={{1,2},{3,4},{5,6},{2,1},{4,3},{6,5},{9,10},{11,12},{13,14},{10,9},... | collective-permute-start | bytes 589832 | tf_op jit(solution)/shard_map/ppermute | solution.py:48
  7.1 10.2 %collective-permute-start.2 = (f32[8,24,256]{2,1,0:T(8,128)S(1)}, f32[8,24,256]{2,1,0:T(8,128)S(1)}, u32[]{:S(2)}, u32[]{:S(2)}) collective-permute-start(f32[8,24,256]{2,1,0:T(8,128)S(1)} %get-tuple-element.24), channel_id=1, source_target_pairs={{0,1},{2,3},{4,5},{6,7},{1,0},{3,2},{5,4},{7,6},{8,9},{10,11},{12,... | collective-permute-start | bytes 589832 | tf_op jit(solution)/shard_map/ppermute | solution.py:48
  15.9 15.6 %collective-permute-start = (f32[224,256]{1,0:T(8,128)S(1)}, f32[224,256]{1,0:T(8,128)S(1)}, u32[]{:S(2)}, u32[]{:S(2)}) collective-permute-start(f32[224,256]{1,0:T(8,128)S(1)} %early.1), channel_id=1, source_target_pairs={{0,8},{8,16},{16,24},{24,32},{32,40},{40,48},{48,56},{56,64},{64,7... | collective-permute-start | bytes 688136 | tf_op jit(solution)/shard_map/ppermute | solution.py:43
  17.8 24.1 %collective-permute-start.4 = (f32[176,256]{1,0:T(8,128)S(1)}, f32[176,256]{1,0:T(8,128)S(1)}, u32[]{:S(2)}, u32[]{:S(2)}) collective-permute-start(f32[176,256]{1,0:T(8,128)S(1)} %get-tuple-element.26), channel_id=1, source_target_pairs={{8,0},{16,8},{24,16},{32,24},{40,32},{48,40},{56,48},{64,56},{72,6... | collective-permute-start | bytes 540680 | tf_op jit(solution)/shard_map/ppermute | solution.py:43
  19.1 12.5 %collective-permute-start.3 = (f32[32,256]{1,0:T(8,128)S(1)}, f32[32,256]{1,0:T(8,128)S(1)}, u32[]{:S(2)}, u32[]{:S(2)}) collective-permute-start(f32[32,256]{1,0:T(8,128)S(1)} %get-tuple-element.25), channel_id=1, source_target_pairs={{0,8},{8,16},{16,24},{24,32},{32,40},{40,48},{48,56},{56,64},{64,7... | collective-permute-start | bytes 98312 | tf_op jit(solution)/shard_map/ppermute | solution.py:43
  27.0 14.9 %copy-start.6 = (s32[32,256]{1,0:T(8,128)S(1)}, s32[32,256]{1,0:T(8,128)}, u32[]{:S(2)}) copy-start(s32[32,256]{1,0:T(8,128)} %ow.1) | copy-start | bytes 98308
  63.4 18.9 %all-to-all-start.1 = ((f32[32,1,128]{2,1,0:T(1,128)}), f32[32,1,128]{2,1,0:T(1,128)S(1)}, u32[]{:S(2)}, u32[]{:S(2)}) async-start(f32[32,1,128]{2,1,0:T(1,128)} %broadcast_in_dim.2), calls=%async_computation.1 | async-start | bytes 32768 | tf_op jit(solution)/shard_map/all_to_all | solution.py:540
